TPU v7x, 32 devices: a whole 2x2x4 slice. The times are simulated.
32 devices in a mesh: ctx: 8 (over y, x, core), fsdp: 4 (over z).
Axes of the slice: x: 2, y: 2, z: 4, core: 2. Of those that a mesh axis runs over, the one named last changes fastest.
Arguments:
- inputs: bfloat16 [4, 3072, 1024], P('fsdp', 'ctx'), may hold values from -6 to 6
- cotangent: bfloat16 [4, 3072, 1024], P('fsdp', 'ctx'), may hold values from -6 to 6
- lengths: int32 [4, 6], P('fsdp'), may hold values from 1 to 1536, 2688 in all within a row
- piece_route: int32 [4, 8, 8], P('fsdp', 'ctx'), may hold values from 0 to 7, each once within a row
- gain_one: bfloat16 [1024], P('fsdp'), may hold values from 0.5 to 1.5
- qkv_weight: bfloat16 [1024, 3072], P('fsdp'), may hold values from -0.1875 to 0.1875
- attn_out: bfloat16 [1024, 1024], P('fsdp'), may hold values from -1.5 to 1.5
- gain_two: bfloat16 [1024], P('fsdp'), may hold values from 0.5 to 1.5
- geglu_in: bfloat16 [1024, 5248], P('fsdp'), may hold values from -0.1875 to 0.1875
- geglu_out: bfloat16 [2624, 1024], P('fsdp'), may hold values from -0.15625 to 0.15625
Outputs:
- block_out: bfloat16 [4, 3072, 1024], P('fsdp', 'ctx')
- grad_inputs: bfloat16 [4, 3072, 1024], P('fsdp', 'ctx')
- grad_gain_one: float32 [1024], P('fsdp')
- grad_qkv_weight: float32 [1024, 3072], P('fsdp')
- grad_attn_out: float32 [1024, 1024], P('fsdp')
- grad_gain_two: float32 [1024], P('fsdp')
- grad_geglu_in: float32 [1024, 5248], P('fsdp')
- grad_geglu_out: float32 [2624, 1024], P('fsdp')
- rms_stats: float32 [4, 3], P('fsdp')
Inputs may be any that keep to these rules, and one draw needn't show every extreme that they name: In each pack the 6 lengths sum to 2688 and the largest is 1536. Each row piece_route[b, s, :] names every index of ctx exactly once.
All inputs are finite; a program needn't handle non-finite values.
Results may differ from a plain program's by a relative error of at most 0.02.
Values may be sent and summed in bfloat16 or wider, within the bound.
A program may use at most 192 MiB of HBM per device.

v0:
```python
import math

import jax
import jax.numpy as jnp
from jax import lax
from jax.sharding import PartitionSpec as P

HEADS = 16


rope_base = 160000.0
norm_eps = 1e-05
masked_score = -1e30


def layer_norm(rows_in, gain_vec):
    row_mean = jnp.mean(rows_in, axis=-1, keepdims=True)
    centred = rows_in - row_mean
    variance = jnp.mean(centred * centred, axis=-1, keepdims=True)
    return centred * lax.rsqrt(variance + norm_eps) * gain_vec


def rotate(projected, places, head_count):
    row_count = projected.shape[0]
    head_width = projected.shape[1] // head_count
    half_width = head_width // 2
    inverse_freq = rope_base ** (-2.0 * jnp.arange(half_width, dtype=jnp.float32) / head_width)
    angles = places.astype(jnp.float32)[:, None] * inverse_freq[None, :]
    cosine = jnp.concatenate([jnp.cos(angles), jnp.cos(angles)], axis=1)[:, None, :]
    sine_table = jnp.concatenate([jnp.sin(angles), jnp.sin(angles)], axis=1)[:, None, :]
    by_head = projected.reshape(row_count, head_count, head_width)
    turned = jnp.concatenate([-by_head[..., half_width:], by_head[..., :half_width]], axis=-1)
    return (by_head * cosine + turned * sine_table).reshape(row_count, head_count * head_width)


def describe(places, lengths_row):
    seq_ends = jnp.cumsum(lengths_row)
    past_end = (places[:, None] >= seq_ends[None, :]).astype(jnp.int32)
    segment = jnp.sum(past_end, axis=1)
    offset = places - jnp.sum(past_end * lengths_row[None, :], axis=1)
    is_valid = places < seq_ends[-1]
    return (segment, offset, is_valid)


def row_table(first_row, block_rows, lengths_row):
    return describe(first_row + jnp.arange(block_rows, dtype=jnp.int32), lengths_row)


def pair_mask(query_segment, query_valid, key_segment, key_valid):
    return (
        (query_segment[:, None] == key_segment[None, :]) & query_valid[:, None] & key_valid[None, :]
    )


def block_scores(queries, key_rows, allowed):
    score_scale = 1.0 / math.sqrt(queries.shape[-1])
    scores = (
        jnp.einsum("qhe,khe->hqk", queries, key_rows, preferred_element_type=jnp.float32)
        * score_scale
    )
    return jnp.where(allowed[None], scores, masked_score)


def block_grads(queries, key_rows, value_rows, grad_heads, log_total, row_delta, allowed):
    masked = block_scores(queries, key_rows, allowed)
    attn_probs = jnp.where(allowed[None], jnp.exp(masked - log_total[:, :, None]), 0.0)
    grad_probs = jnp.einsum(
        "qhe,khe->hqk", grad_heads, value_rows, preferred_element_type=jnp.float32
    )
    grad_scores = (attn_probs * (grad_probs - row_delta[:, :, None])).astype(jnp.bfloat16)
    return (attn_probs.astype(jnp.bfloat16), grad_scores)


def key_slice(
    key_all, value_all, block_index, key_block, query_segment, query_valid, lengths_row, head_count
):
    first_row = block_index * key_block
    head_width = key_all.shape[1] // head_count
    key_rows = lax.dynamic_slice_in_dim(key_all, first_row, key_block, 0).reshape(
        key_block, head_count, head_width
    )
    value_rows = lax.dynamic_slice_in_dim(value_all, first_row, key_block, 0).reshape(
        key_block, head_count, head_width
    )
    key_segment, unused_offset, key_valid = row_table(first_row, key_block, lengths_row)
    return (key_rows, value_rows, pair_mask(query_segment, query_valid, key_segment, key_valid))


def attention_forward(queries, key_all, value_all, query_segment, query_valid, lengths_row):
    row_count, head_count, head_width = queries.shape
    key_block = math.gcd(key_all.shape[0], 512)
    block_count = key_all.shape[0] // key_block

    def first_pass(block_index, carried):
        key_rows, value_rows, allowed = key_slice(
            key_all,
            value_all,
            block_index,
            key_block,
            query_segment,
            query_valid,
            lengths_row,
            head_count,
        )

        def first_work(state_in):
            running_top, weight_sum = state_in
            masked = block_scores(queries, key_rows, allowed)
            new_top = jnp.maximum(running_top, jnp.max(masked, axis=-1))
            fresh = jnp.where(allowed[None], jnp.exp(masked - new_top[:, :, None]), 0.0)
            return (new_top, weight_sum * jnp.exp(running_top - new_top) + jnp.sum(fresh, axis=-1))

        return lax.cond(jnp.any(allowed), first_work, lambda state_in: state_in, carried)

    start_top = jnp.full((head_count, row_count), masked_score, jnp.float32)
    start_sum = jnp.zeros((head_count, row_count), jnp.float32)
    running_top, weight_sum = lax.fori_loop(0, block_count, first_pass, (start_top, start_sum))
    log_total = running_top + jnp.log(weight_sum + jnp.where(query_valid, 0.0, 1.0)[None, :])

    def second_pass(block_index, carried):
        key_rows, value_rows, allowed = key_slice(
            key_all,
            value_all,
            block_index,
            key_block,
            query_segment,
            query_valid,
            lengths_row,
            head_count,
        )

        def second_work(acc_in):
            masked = block_scores(queries, key_rows, allowed)
            probs_low = jnp.where(
                allowed[None], jnp.exp(masked - log_total[:, :, None]), 0.0
            ).astype(jnp.bfloat16)
            return acc_in + jnp.einsum(
                "hqk,khe->qhe", probs_low, value_rows, preferred_element_type=jnp.float32
            )

        return lax.cond(jnp.any(allowed), second_work, lambda acc_in: acc_in, carried)

    attended = lax.fori_loop(
        0, block_count, second_pass, jnp.zeros((row_count, head_count, head_width), jnp.float32)
    )
    return (attended.reshape(row_count, head_count * head_width), log_total)


def query_grads(
    queries,
    key_all,
    value_all,
    grad_heads,
    log_total,
    row_delta,
    query_segment,
    query_valid,
    lengths_row,
):
    row_count, head_count, head_width = queries.shape
    score_scale = 1.0 / math.sqrt(head_width)
    key_total = key_all.shape[0]
    key_block = math.gcd(key_total, 512)
    block_count = key_total // key_block

    def step_back(block_index, carried):
        key_rows, value_rows, allowed = key_slice(
            key_all,
            value_all,
            block_index,
            key_block,
            query_segment,
            query_valid,
            lengths_row,
            head_count,
        )

        def step_work(state_in):
            grad_query_in, buffer_in = state_in
            probs_low, grad_scores = block_grads(
                queries, key_rows, value_rows, grad_heads, log_total, row_delta, allowed
            )
            grad_query_in = (
                grad_query_in
                + jnp.einsum(
                    "hqk,khe->qhe", grad_scores, key_rows, preferred_element_type=jnp.float32
                )
                * score_scale
            )
            grad_key = (
                jnp.einsum("hqk,qhe->khe", grad_scores, queries, preferred_element_type=jnp.float32)
                * score_scale
            )
            grad_value = jnp.einsum(
                "hqk,qhe->khe", probs_low, grad_heads, preferred_element_type=jnp.float32
            )
            joined = jnp.concatenate(
                [grad_key.reshape(key_block, -1), grad_value.reshape(key_block, -1)], axis=1
            )
            buffer_in = lax.dynamic_update_slice_in_dim(
                buffer_in, joined, block_index * key_block, 0
            )
            return (grad_query_in, buffer_in)

        return lax.cond(jnp.any(allowed), step_work, lambda state_in: state_in, carried)

    start_buffer = jnp.zeros((key_total, 2 * head_count * head_width), jnp.float32)
    start_query = jnp.zeros((row_count, head_count, head_width), jnp.float32)
    return lax.fori_loop(0, block_count, step_back, (start_query, start_buffer))


def per_device(
    inputs,
    cotangent,
    lengths,
    piece_route,
    gain_one,
    qkv_weight,
    attn_out,
    gain_two,
    geglu_in,
    geglu_out,
):
    ctx_count = lax.axis_size("ctx")
    own_index = lax.axis_index("ctx")
    row_count = inputs.shape[1]
    model_width = inputs.shape[2]
    piece_rows = row_count // ctx_count
    head_width = model_width // HEADS
    lengths_row = lengths[0]
    own_route = piece_route[0, 0]
    slot_ids = jnp.arange(ctx_count, dtype=jnp.int32)
    outgoing = jnp.sum(
        slot_ids[None, :] * (own_route[None, :] == slot_ids[:, None]).astype(jnp.int32), axis=1
    )

    def to_slots(rows_in):
        return jnp.take(rows_in.reshape(ctx_count, piece_rows, model_width), outgoing, axis=0)

    arrived, grad_arrived = (
        lax.all_to_all(to_slots(inputs[0]), "ctx", split_axis=0, concat_axis=0, tiled=True),
        lax.all_to_all(to_slots(cotangent[0]), "ctx", split_axis=0, concat_axis=0, tiled=True),
    )
    residual = arrived.reshape(row_count, model_width).astype(jnp.float32)
    places = own_index * row_count + jnp.arange(row_count, dtype=jnp.int32)
    segment, offset, is_valid = describe(places, lengths_row)
    grad_final = jnp.where(
        is_valid[:, None], grad_arrived.reshape(row_count, model_width).astype(jnp.float32), 0.0
    )
    gain_attn_low, qkv_full, attn_full = (
        lax.all_gather(gain_one, "fsdp", axis=0, tiled=True),
        lax.all_gather(qkv_weight, "fsdp", axis=0, tiled=True),
        lax.all_gather(attn_out, "fsdp", axis=0, tiled=True),
    )
    gain_attn = gain_attn_low.astype(jnp.float32)
    act_attn = layer_norm(residual, gain_attn).astype(jnp.bfloat16)
    projected = jnp.dot(act_attn, qkv_full, preferred_element_type=jnp.float32)
    queries = rotate(projected[:, :model_width], offset, HEADS).astype(jnp.bfloat16)
    key_local = rotate(projected[:, model_width : 2 * model_width], offset, HEADS).astype(
        jnp.bfloat16
    )
    value_local = projected[:, 2 * model_width :].astype(jnp.bfloat16)
    key_all, value_all = (
        lax.all_gather(key_local, "ctx", axis=0, tiled=True),
        lax.all_gather(value_local, "ctx", axis=0, tiled=True),
    )
    query_heads = queries.reshape(row_count, HEADS, head_width)
    attended, log_total = attention_forward(
        query_heads, key_all, value_all, segment, is_valid, lengths_row
    )
    attn_low = attended.astype(jnp.bfloat16)
    branch_attn = jnp.dot(attn_low, attn_full, preferred_element_type=jnp.float32)
    middle = residual + branch_attn
    gain_mlp_low, in_full, out_full = (
        lax.all_gather(gain_two, "fsdp", axis=0, tiled=True),
        lax.all_gather(geglu_in, "fsdp", axis=0, tiled=True),
        lax.all_gather(geglu_out, "fsdp", axis=0, tiled=True),
    )
    gain_mlp = gain_mlp_low.astype(jnp.float32)
    act_mlp = layer_norm(middle, gain_mlp).astype(jnp.bfloat16)
    up_both = jnp.dot(act_mlp, in_full, preferred_element_type=jnp.float32)
    ff_width = up_both.shape[1] // 2
    hidden = (jax.nn.gelu(up_both[:, :ff_width], approximate=False) * up_both[:, ff_width:]).astype(
        jnp.bfloat16
    )
    branch_mlp = jnp.dot(hidden, out_full, preferred_element_type=jnp.float32)
    final_rows = jnp.where(is_valid[:, None], middle + branch_mlp, 0.0)
    square_sums = jnp.stack(
        [
            jnp.sum(final_rows * final_rows),
            jnp.sum(jnp.where(is_valid[:, None], branch_attn * branch_attn, 0.0)),
            jnp.sum(jnp.where(is_valid[:, None], branch_mlp * branch_mlp, 0.0)),
        ]
    )
    gain_mlp_low, in_full, out_full = (
        lax.all_gather(gain_two, "fsdp", axis=0, tiled=True),
        lax.all_gather(geglu_in, "fsdp", axis=0, tiled=True),
        lax.all_gather(geglu_out, "fsdp", axis=0, tiled=True),
    )
    gain_mlp = gain_mlp_low.astype(jnp.float32)
    grad_mlp_low = grad_final.astype(jnp.bfloat16)
    grad_out_mlp = jnp.dot(hidden.T, grad_mlp_low, preferred_element_type=jnp.float32)
    grad_hidden = jnp.dot(grad_mlp_low, out_full.T, preferred_element_type=jnp.float32)

    def gated(leading, trailing):
        return jax.nn.gelu(leading, approximate=False) * trailing

    unused_gate, gate_back = jax.vjp(gated, up_both[:, :ff_width], up_both[:, ff_width:])
    grad_leading, grad_trailing = gate_back(grad_hidden)
    grad_up = jnp.concatenate([grad_leading, grad_trailing], axis=1).astype(jnp.bfloat16)
    grad_in_mlp = jnp.dot(act_mlp.T, grad_up, preferred_element_type=jnp.float32)
    grad_act_mlp = jnp.dot(grad_up, in_full.T, preferred_element_type=jnp.float32)
    unused_norm, norm_back_mlp = jax.vjp(layer_norm, middle, gain_mlp)
    grad_middle_norm, grad_gain_mlp = norm_back_mlp(grad_act_mlp)
    grad_middle = grad_final + grad_middle_norm
    gain_attn_low, qkv_full, attn_full = (
        lax.all_gather(gain_one, "fsdp", axis=0, tiled=True),
        lax.all_gather(qkv_weight, "fsdp", axis=0, tiled=True),
        lax.all_gather(attn_out, "fsdp", axis=0, tiled=True),
    )
    gain_attn = gain_attn_low.astype(jnp.float32)
    key_all, value_all = (
        lax.all_gather(key_local, "ctx", axis=0, tiled=True),
        lax.all_gather(value_local, "ctx", axis=0, tiled=True),
    )
    grad_attn_low = grad_middle.astype(jnp.bfloat16)
    grad_attn_proj = jnp.dot(attn_low.T, grad_attn_low, preferred_element_type=jnp.float32)
    grad_attended = jnp.dot(grad_attn_low, attn_full.T, preferred_element_type=jnp.float32).astype(
        jnp.bfloat16
    )
    grad_heads = grad_attended.reshape(row_count, HEADS, head_width)
    row_delta = jnp.sum(
        grad_heads.astype(jnp.float32) * attended.reshape(row_count, HEADS, head_width), axis=-1
    ).T
    grad_query, key_buffer = query_grads(
        query_heads,
        key_all,
        value_all,
        grad_heads,
        log_total,
        row_delta,
        segment,
        is_valid,
        lengths_row,
    )
    key_terms = lax.psum_scatter(
        key_buffer.astype(jnp.bfloat16), "ctx", scatter_dimension=0, tiled=True
    ).astype(jnp.float32)
    grad_key = key_terms[:, :model_width]
    grad_value = key_terms[:, model_width:]

    def rotate_here(rows_in):
        return rotate(rows_in, offset, HEADS)

    unused_turn, rotate_back = jax.vjp(rotate_here, projected[:, :model_width])
    grad_query_pre = rotate_back(grad_query.reshape(row_count, model_width))[0]
    grad_key_pre = rotate_back(grad_key)[0]
    grad_projected = jnp.concatenate([grad_query_pre, grad_key_pre, grad_value], axis=1).astype(
        jnp.bfloat16
    )
    grad_qkv_full = jnp.dot(act_attn.T, grad_projected, preferred_element_type=jnp.float32)
    grad_act_attn = jnp.dot(grad_projected, qkv_full.T, preferred_element_type=jnp.float32)
    unused_first, norm_back_attn = jax.vjp(layer_norm, residual, gain_attn)
    grad_resid_norm, grad_gain_attn = norm_back_attn(grad_act_attn)
    grad_residual = (grad_middle + grad_resid_norm).astype(jnp.bfloat16)
    out_slots = final_rows.astype(jnp.bfloat16).reshape(ctx_count, piece_rows, model_width)
    grad_slots = grad_residual.reshape(ctx_count, piece_rows, model_width)
    back_out, back_grad = (
        lax.all_to_all(out_slots, "ctx", split_axis=0, concat_axis=0, tiled=True),
        lax.all_to_all(grad_slots, "ctx", split_axis=0, concat_axis=0, tiled=True),
    )
    block_out = jnp.take(back_out, own_route, axis=0).reshape(1, row_count, model_width)
    grad_inputs = jnp.take(back_grad, own_route, axis=0).reshape(1, row_count, model_width)
    shard_gain_one, shard_qkv, shard_attn, shard_gain_two, shard_in, shard_out = (
        lax.psum_scatter(
            grad_gain_attn.astype(jnp.bfloat16), "fsdp", scatter_dimension=0, tiled=True
        ).astype(jnp.float32),
        lax.psum_scatter(
            grad_qkv_full.astype(jnp.bfloat16), "fsdp", scatter_dimension=0, tiled=True
        ).astype(jnp.float32),
        lax.psum_scatter(
            grad_attn_proj.astype(jnp.bfloat16), "fsdp", scatter_dimension=0, tiled=True
        ).astype(jnp.float32),
        lax.psum_scatter(
            grad_gain_mlp.astype(jnp.bfloat16), "fsdp", scatter_dimension=0, tiled=True
        ).astype(jnp.float32),
        lax.psum_scatter(
            grad_in_mlp.astype(jnp.bfloat16), "fsdp", scatter_dimension=0, tiled=True
        ).astype(jnp.float32),
        lax.psum_scatter(
            grad_out_mlp.astype(jnp.bfloat16), "fsdp", scatter_dimension=0, tiled=True
        ).astype(jnp.float32),
    )
    total_gain_one, total_qkv, total_attn, total_gain_two, total_in, total_out, total_squares = (
        lax.psum(shard_gain_one.astype(jnp.bfloat16), "ctx").astype(jnp.float32),
        lax.psum(shard_qkv.astype(jnp.bfloat16), "ctx").astype(jnp.float32),
        lax.psum(shard_attn.astype(jnp.bfloat16), "ctx").astype(jnp.float32),
        lax.psum(shard_gain_two.astype(jnp.bfloat16), "ctx").astype(jnp.float32),
        lax.psum(shard_in.astype(jnp.bfloat16), "ctx").astype(jnp.float32),
        lax.psum(shard_out.astype(jnp.bfloat16), "ctx").astype(jnp.float32),
        lax.psum(square_sums.astype(jnp.bfloat16), "ctx").astype(jnp.float32),
    )
    valid_count = jnp.sum(lengths_row).astype(jnp.float32)
    rms_stats = jnp.sqrt(total_squares / (valid_count * model_width))[None, :]
    return (
        block_out,
        grad_inputs,
        total_gain_one,
        total_qkv,
        total_attn,
        total_gain_two,
        total_in,
        total_out,
        rms_stats,
    )


def solution(mesh):
    placed = (
        P("fsdp", "ctx", None),
        P("fsdp", "ctx", None),
        P("fsdp", None),
        P("fsdp", "ctx", None),
        P("fsdp"),
        P("fsdp", None),
        P("fsdp", None),
        P("fsdp"),
        P("fsdp", None),
        P("fsdp", None),
    )
    return jax.shard_map(
        per_device,
        mesh=mesh,
        in_specs=placed,
        out_specs=(
            P("fsdp", "ctx", None),
            P("fsdp", "ctx", None),
            P("fsdp"),
            P("fsdp", None),
            P("fsdp", None),
            P("fsdp"),
            P("fsdp", None),
            P("fsdp", None),
            P("fsdp", None),
        ),
        check_vma=False,
    )
```

profile of v0, /device:TPU:1, one launch (start us, length us, event | category | flops | bytes accessed | tf_op | source)
XLA Modules:
  0.0 1527.0 jit_solution(11550804361712979456)
XLA Ops:
  11.3 5.2 all-to-all-start
  16.6 9.3 all-gather
  30.8 96.4 %all-gather.9.cloned.1.call-done = bf16[1024,3072]{1,0:T(8,128)(2,1)} async-done(((bf16[256,3072]{1,0:T(8,128)(2,1)}), bf16[1024,3072]{1,0:T(8,128)(2,1)}) %all-gather.9.cloned.1.call-update) | async-done | bytes 6291472 | tf_op jit(solution)/shard_map/all_gather | solution.py:252
  166.2 6.3 all-gather.1
  173.1 7.5 all-to-all-done.2
  182.2 26.1 %all-gather.11.cloned.1.call-done = bf16[3072,1024]{1,0:T(8,128)(2,1)} async-done(((bf16[384,1024]{1,0:T(8,128)(2,1)}), bf16[3072,1024]{1,0:T(8,128)(2,1)}) %all-gather.11.cloned.1.call-update) | async-done | bytes 6291472 | tf_op jit(solution)/shard_map/all_gather | solution.py:264
  208.3 8.6 copy.89
  216.9 47.0 %while.55 = (s32[]{:T(128)}, f32[16,384]{1,0:T(8,128)S(1)}, f32[16,384]{1,0:T(8,128)S(1)}, s32[384]{0:T(512)S(1)}, s32[6,1]{0,1:T(1,128)S(1)}, /*index=5*/bf16[3...) while((s32[]{:T(128)}, f32[16,384]{1,0:T(8,128)S(1)}, ...), condition=%wide.region_13.15_spmd.clone, body=%wide.region_6.14_spmd.clone.sunk | while | flops 428628736 | bytes 30019120 | solution.py:117
  220.4 6.5 conditional.9
  230.4 6.5 conditional.9
  240.4 6.5 conditional.9
  250.4 6.5 conditional.9
  264.0 8.7 copy.90
  274.0 60.0 %while.56 = (s32[]{:T(128)}, f32[384,16,64]{0,2,1:T(8,128)}, s32[384]{0:T(512)S(1)}, s32[6,1]{0,1:T(1,128)S(1)}, bf16[3072,1024]{0,1:T(8,128)(2,1)}, /*index=5*/...) while((s32[]{:T(128)}, f32[384,16,64]{0,2,1:T(8,128)}, ...), condition=%wide.region_19.21_spmd.clone, body=%wide.region_14.20_spmd.clone.sunk | while | flops 822225664 | bytes 10653217 | solution.py:143
  277.5 9.8 conditional.10
  280.2 7.0 bitcast_add_fusion
  290.8 9.7 conditional.10
  293.4 7.0 bitcast_add_fusion
  303.9 9.7 conditional.10
  306.6 7.0 bitcast_add_fusion
  317.1 9.9 conditional.10
  320.0 7.0 bitcast_add_fusion
  340.8 150.7 %all-gather.17.cloned.1.call-done = bf16[1024,5248]{1,0:T(8,128)(2,1)} async-done(((bf16[256,5248]{1,0:T(8,128)(2,1)}), bf16[1024,5248]{1,0:T(8,128)(2,1)}) %all-gather.17.cloned.1.call-update) | async-done | bytes 10747920 | tf_op jit(solution)/shard_map/all_gather | solution.py:276
  491.5 11.2 fusion.67
  502.7 88.5 %all-gather.19.cloned.1.call-done = bf16[2624,1024]{1,0:T(8,128)(2,1)} async-done(((bf16[656,1024]{1,0:T(8,128)(2,1)}), bf16[2624,1024]{1,0:T(8,128)(2,1)}) %all-gather.19.cloned.1.call-update) | async-done | bytes 5373968 | tf_op jit(solution)/shard_map/all_gather | solution.py:277
  591.2 16.1 %add_convert_fusion = (bf16[384,2624]{1,0:T(8,128)(2,1)}, f32[384,2624]{1,0:T(8,128)}, f32[384,2624]{1,0:T(8,128)}) fusion(f32[384,5248]{1,0:T(8,128)} %fusion.67, bf16[384,1024]{1,0:T(8,128)(2,1)S(1)} %copy-done.29, bf16[2624,1024]{1,0:T(8,128)(2,1)} %all-gather.19.cloned.1.call-done), kind=kOutput, calls=%fused_computation.64 | convolution fusion | flops 2137153536 | bytes 24297472 | tf_op jit(solution)/shard_map/dot_general | solution.py:303
  607.3 7.1 multiply_convert_fusion
  614.4 8.7 fusion.39
  623.1 6.9 multiply_reduce_fusion
  637.1 6.1 broadcast_in_dim.237
  644.5 164.5 %while.57 = (s32[]{:T(128)}, f32[384,16,64]{0,2,1:T(8,128)}, bf16[3072,2048]{0,1:T(8,128)(2,1)}, s32[384]{0:T(512)S(1)}, s32[6,1]{0,1:T(1,128)S(1)}, /*index=5*/...) while((s32[]{:T(128)}, f32[384,16,64]{0,2,1:T(8,128)}, ...), condition=%wide.region_30.32_spmd.clone, body=%wide.region_25.31_spmd.clone.sunk | while | flops 2057841408 | bytes 102387392 | solution.py:209
  648.1 35.8 %conditional.11 = ((f32[384,16,64]{0,2,1:T(8,128)}, bf16[3072,2048]{0,1:T(8,128)(2,1)})) conditional(s32[]{:T(128)} %convert_element_type.331, (f32[384,16,64]{0,2,1:T(8,128)}, bf16[3072,2048]{0,1:T(8,128)(2,1)}) %tuple.224, (pred[384,512]{0,1:T(8,128)(4,1)S(1)}, s32[]{:T(128)}, bf16[3072,1024]{0,1:T(8,128)(2,1)}, ...), branch_computations={%region_28.29_spmd, %region_29.30_spmd} | conditional | flops 2057043968 | bytes 102178952 | solution.py:205
  649.8 6.4 fusion.79
  656.3 7.5 fusion.21
  666.5 9.1 fusion.26
  678.4 5.5 bitcast_add_fusion.1
  687.4 35.9 %conditional.11 = ((f32[384,16,64]{0,2,1:T(8,128)}, bf16[3072,2048]{0,1:T(8,128)(2,1)})) conditional(s32[]{:T(128)} %convert_element_type.331, (f32[384,16,64]{0,2,1:T(8,128)}, bf16[3072,2048]{0,1:T(8,128)(2,1)}) %tuple.224, (pred[384,512]{0,1:T(8,128)(4,1)S(1)}, s32[]{:T(128)}, bf16[3072,1024]{0,1:T(8,128)(2,1)}, ...), branch_computations={%region_28.29_spmd, %region_29.30_spmd} | conditional | flops 2057043968 | bytes 102178952 | solution.py:205
  689.1 6.4 fusion.79
  695.6 7.5 fusion.21
  705.8 9.1 fusion.26
  717.8 5.5 bitcast_add_fusion.1
  726.8 35.8 %conditional.11 = ((f32[384,16,64]{0,2,1:T(8,128)}, bf16[3072,2048]{0,1:T(8,128)(2,1)})) conditional(s32[]{:T(128)} %convert_element_type.331, (f32[384,16,64]{0,2,1:T(8,128)}, bf16[3072,2048]{0,1:T(8,128)(2,1)}) %tuple.224, (pred[384,512]{0,1:T(8,128)(4,1)S(1)}, s32[]{:T(128)}, bf16[3072,1024]{0,1:T(8,128)(2,1)}, ...), branch_computations={%region_28.29_spmd, %region_29.30_spmd} | conditional | flops 2057043968 | bytes 102178952 | solution.py:205
  728.5 6.4 fusion.79
  735.0 7.5 fusion.21
  745.2 9.1 fusion.26
  757.1 5.5 bitcast_add_fusion.1
  766.1 35.8 %conditional.11 = ((f32[384,16,64]{0,2,1:T(8,128)}, bf16[3072,2048]{0,1:T(8,128)(2,1)})) conditional(s32[]{:T(128)} %convert_element_type.331, (f32[384,16,64]{0,2,1:T(8,128)}, bf16[3072,2048]{0,1:T(8,128)(2,1)}) %tuple.224, (pred[384,512]{0,1:T(8,128)(4,1)S(1)}, s32[]{:T(128)}, bf16[3072,1024]{0,1:T(8,128)(2,1)}, ...), branch_computations={%region_28.29_spmd, %region_29.30_spmd} | conditional | flops 2057043968 | bytes 102178952 | solution.py:205
  767.8 6.4 fusion.79
  774.3 7.5 fusion.21
  784.5 9.1 fusion.26
  796.4 5.5 bitcast_add_fusion.1
  809.0 15.8 %copy.101 = bf16[3072,2048]{1,0:T(8,128)(2,1)} copy(bf16[3072,2048]{0,1:T(8,128)(2,1)} %get-tuple-element.989) | data formatting | bytes 25165824
  829.9 6.5 convolution_convert_fusion.1
  837.9 11.2 convolution_convert_fusion
  849.1 101.9 %reduce-scatter.16.cloned.1.call-done = bf16[384,2048]{1,0:T(8,128)(2,1)} async-done(((bf16[3072,2048]{1,0:T(8,128)(2,1)}), bf16[384,2048]{1,0:T(8,128)(2,1)}) %reduce-scatter.16.cloned.1.call-update) | async-done | bytes 1572880
  958.9 8.5 convolution_convert_fusion.2
  972.0 25.3 %reduce-scatter.10.cloned.1.call-done = bf16[256,1024]{1,0:T(8,128)(2,1)} async-done(((bf16[1024,1024]{1,0:T(8,128)(2,1)}), bf16[256,1024]{1,0:T(8,128)(2,1)}) %reduce-scatter.10.cloned.1.call-update) | async-done | bytes 524304 | tf_op jit(solution)/shard_map/reduce_scatter | solution.py:381
  997.3 98.4 %reduce-scatter.14.cloned.1.call-done = bf16[656,1024]{1,0:T(8,128)(2,1)} async-done(((bf16[2624,1024]{1,0:T(8,128)(2,1)}), bf16[656,1024]{1,0:T(8,128)(2,1)}) %reduce-scatter.14.cloned.1.call-update) | async-done | bytes 1343504 | tf_op jit(solution)/shard_map/reduce_scatter | solution.py:390
  1095.7 185.0 %reduce-scatter.12.cloned.1.call-done = bf16[256,5248]{1,0:T(8,128)(2,1)} async-done(((bf16[1024,5248]{1,0:T(8,128)(2,1)}), bf16[256,5248]{1,0:T(8,128)(2,1)}) %reduce-scatter.12.cloned.1.call-update) | async-done | bytes 2686992 | tf_op jit(solution)/shard_map/reduce_scatter | solution.py:387
  1280.7 114.2 %reduce-scatter.8.cloned.1.call-done = bf16[256,3072]{1,0:T(8,128)(2,1)} async-done(((bf16[1024,3072]{1,0:T(8,128)(2,1)}), bf16[256,3072]{1,0:T(8,128)(2,1)}) %reduce-scatter.8.cloned.1.call-update) | async-done | bytes 1572880 | tf_op jit(solution)/shard_map/reduce_scatter | solution.py:378
  1395.0 6.0 fusion.52
  1413.6 9.2 all-reduce.8
  1422.9 14.2 all-reduce.6
  1440.7 69.4 %all-reduce.11.cloned.1.call-done = (bf16[256,3072]{1,0:T(8,128)(2,1)}, bf16[256,1024]{1,0:T(8,128)(2,1)}, bf16[256,5248]{1,0:T(8,128)(2,1)}, bf16[656,1024]{1,0:T(8,128)(2,1)}) async-done(((bf16[256,3072]{1,0:T(8,128)(2,1)}, bf16[256,1024]{1,0:T(8,128)(2,1)}, bf16[256,5248]{1,0:T(8,128)(2,1)}, bf16[656,1024]{1,0:T(8,128)(2,1)}), (bf16[256,3072]{1,0:T(8,128)(2,1)}, bf16[256,1024]{1,0:T(8,128)(2,1)}, ...) | async-done | bytes 6127632 | tf_op jit(solution)/shard_map/psum | solution.py:396
  (397 shorter events, 225.6 us)
Async XLA Ops:
  7.2 2.2 copy-start.26
  7.2 120.0 %all-gather.9.cloned.1.call-start = ((), (), s32[]{:S(2)}) async-start(), calls=%async_computation.9 | async-start | bytes 7864320 | tf_op jit(solution)/shard_map/all_gather | solution.py:252
  9.4 7.2 copy-start.54
  9.4 16.6 %copy-start.52 = (s32[1,6]{1,0:T(1,128)S(1)}, s32[1,6]{1,0:T(1,128)}, u32[]{:S(2)}) copy-start(s32[1,6]{1,0:T(1,128)} %param.26) | copy-start | bytes 76
  11.3 18.4 %all-to-all-start = ((bf16[8,48,1024]{2,1,0:T(8,128)(2,1)}), bf16[8,48,1024]{2,1,0:T(8,128)(2,1)S(1)}, u32[]{:S(2)}, u32[]{:S(2)}) async-start(bf16[8,48,1024]{2,1,0:T(8,128)(2,1)} %get-tuple-element.1330), calls=%async_computation | async-start | bytes 1572864 | tf_op jit(solution)/shard_map/all_to_all | solution.py:241
  16.6 191.7 %all-gather.11.cloned.1.call-start = ((), (), s32[]{:S(2)}) async-start(), calls=%async_computation.10 | async-start | bytes 7077888 | tf_op jit(solution)/shard_map/all_gather | solution.py:264
  25.9 4.5 copy-start.39
  26.5 3.9 copy-start.22
  26.5 117.7 %copy-start.24 = (f32[384,64]{0,1:T(8,128)}, f32[384,64]{0,1:T(8,128)S(1)}, u32[]{:S(2)}) copy-start(f32[384,64]{0,1:T(8,128)S(1)} %get-tuple-element.1336) | copy-start | bytes 294916
  29.7 306.7 %copy-start.3 = (bf16[8,48,1024]{2,1,0:T(8,128)(2,1)}, bf16[8,48,1024]{2,1,0:T(8,128)(2,1)S(1)}, u32[]{:S(2)}) copy-start(bf16[8,48,1024]{2,1,0:T(8,128)(2,1)S(1)} %all-to-all-done) | copy-start | bytes 2359300
  30.0 101.9 %copy-start.41 = (f32[384]{0:T(512)}, f32[384]{0:T(512)S(1)}, u32[]{:S(2)}) copy-start(f32[384]{0:T(512)S(1)} %div.56) | copy-start | bytes 4612
  30.5 101.4 %copy-start.47 = (f32[384]{0:T(512)}, f32[384]{0:T(512)S(1)}, u32[]{:S(2)}) copy-start(f32[384]{0:T(512)S(1)} %add.309) | copy-start | bytes 4612
  30.5 101.4 %copy-start.43 = (f32[384]{0:T(512)}, f32[384]{0:T(512)S(1)}, u32[]{:S(2)}) copy-start(f32[384]{0:T(512)S(1)} %rsqrt.22) | copy-start | bytes 4612
  30.8 101.1 %copy-start.27 = (bf16[384,1024]{1,0:T(8,128)(2,1)}, bf16[384,1024]{1,0:T(8,128)(2,1)S(1)}, u32[]{:S(2)}) copy-start(bf16[384,1024]{1,0:T(8,128)(2,1)S(1)} %fusion.50) | copy-start | bytes 2359300
  131.9 2.2 copy-start.12
  157.1 106.9 %all-gather.13.cloned.1.call-start = ((), (), s32[]{:S(2)}) async-start(), calls=%async_computation.11 | async-start | bytes 7077888 | tf_op jit(solution)/shard_map/all_gather | solution.py:265
  159.6 6.6 copy-start.55
  159.6 176.8 %all-gather.15.cloned.1.call-start = ((), (), s32[]{:S(2)}) async-start(), calls=%async_computation.12 | async-start | bytes 2621440 | tf_op jit(solution)/shard_map/all_gather | solution.py:253
  160.2 21.6 %copy-start.14 = (bf16[384,1024]{1,0:T(8,128)(2,1)S(1)}, bf16[384,1024]{1,0:T(8,128)(2,1)}, u32[]{:S(2)}) copy-start(bf16[384,1024]{1,0:T(8,128)(2,1)} %get-tuple-element.1304) | copy-start | bytes 2359300
  160.2 331.3 %all-gather.17.cloned.1.call-start = ((), (), s32[]{:S(2)}) async-start(), calls=%async_computation.13 | async-start | bytes 13434880 | tf_op jit(solution)/shard_map/all_gather | solution.py:276
  160.8 19.9 %all-to-all-start.2 = ((bf16[8,48,1024]{2,1,0:T(8,128)(2,1)}), bf16[8,48,1024]{2,1,0:T(8,128)(2,1)S(1)}, u32[]{:S(2)}, u32[]{:S(2)}) async-start(bf16[8,48,1024]{2,1,0:T(8,128)(2,1)} %get-tuple-element.1329), calls=%async_computation.2 | async-start | bytes 1572864 | tf_op jit(solution)/shard_map/all_to_all | solution.py:242
  165.0 426.2 %all-gather.19.cloned.1.call-start = ((), (), s32[]{:S(2)}) async-start(), calls=%async_computation.14 | async-start | bytes 6717440 | tf_op jit(solution)/shard_map/all_gather | solution.py:277
  165.5 785.5 %reduce-scatter.16.cloned.1.call-start = ((), (), s32[]{:S(2)}) async-start(), calls=%async_computation.19 | async-start | bytes 14155776
  172.5 457.6 %copy-start.33 = (f32[4,1,256]{2,1,0:T(1,128)}, f32[4,1,256]{2,1,0:T(1,128)S(1)}, u32[]{:S(2)}) copy-start(f32[4,1,256]{2,1,0:T(1,128)S(1)} %convert_element_type.250) | copy-start | bytes 12292
  173.1 457.6 %copy-start.49 = (pred[384]{0:T(512)(128)(4,1)}, pred[384]{0:T(512)(128)(4,1)S(1)}, u32[]{:S(2)}) copy-start(pred[384]{0:T(512)(128)(4,1)S(1)} %get-tuple-element.1295) | copy-start | bytes 1156
  340.4 289.6 %copy-start.5 = (f32[384,1024]{1,0:T(8,128)}, f32[384,1024]{1,0:T(8,128)S(1)}, u32[]{:S(2)}) copy-start(f32[384,1024]{1,0:T(8,128)S(1)} %get-tuple-element.1293) | copy-start | bytes 4718596
  340.4 289.6 %copy-start.35 = (f32[384]{0:T(512)}, f32[384]{0:T(512)S(1)}, u32[]{:S(2)}) copy-start(f32[384]{0:T(512)S(1)} %broadcast_multiply_fusion.2) | copy-start | bytes 4612
  340.8 289.3 %copy-start.37 = (f32[384]{0:T(512)}, f32[384]{0:T(512)S(1)}, u32[]{:S(2)}) copy-start(f32[384]{0:T(512)S(1)} %fusion.61) | copy-start | bytes 4612
  491.5 99.7 %copy-start.29 = (bf16[384,1024]{1,0:T(8,128)(2,1)S(1)}, bf16[384,1024]{1,0:T(8,128)(2,1)}, u32[]{:S(2)}) copy-start(bf16[384,1024]{1,0:T(8,128)(2,1)} %fusion.44) | copy-start | bytes 2359300
  591.2 16.1 %copy-start.13 = (f32[384,5248]{1,0:T(8,128)S(1)}, f32[384,5248]{1,0:T(8,128)}, u32[]{:S(2)}) copy-start(f32[384,5248]{1,0:T(8,128)} %fusion.67) | copy-start | bytes 24182788
  614.4 8.7 copy-start.17
  614.4 8.7 copy-start.20
  630.1 2.9 copy-start.16
  630.7 3.4 copy-start.45
  663.8 2.7 copy-start.2
  703.1 2.7 copy-start.2
  742.5 2.7 copy-start.2
  781.8 2.7 copy-start.2
  824.8 5.1 copy-start.18
  824.8 172.5 %reduce-scatter.10.cloned.1.call-start = ((), (), s32[]{:S(2)}) async-start(), calls=%async_computation.16 | async-start | bytes 2621440 | tf_op jit(solution)/shard_map/reduce_scatter | solution.py:381
  829.6 266.0 %reduce-scatter.14.cloned.1.call-start = ((), (), s32[]{:S(2)}) async-start(), calls=%async_computation.18 | async-start | bytes 6717440 | tf_op jit(solution)/shard_map/reduce_scatter | solution.py:390
  836.5 444.2 %reduce-scatter.12.cloned.1.call-start = ((), (), s32[]{:S(2)}) async-start(), calls=%async_computation.17 | async-start | bytes 13434880 | tf_op jit(solution)/shard_map/reduce_scatter | solution.py:387
  849.1 104.9 %copy-start.25 = (f32[384,64]{0,1:T(8,128)S(1)}, f32[384,64]{0,1:T(8,128)}, u32[]{:S(2)}) copy-start(f32[384,64]{0,1:T(8,128)} %copy-done.24) | copy-start | bytes 294916
  849.1 545.8 %reduce-scatter.8.cloned.1.call-start = ((), (), s32[]{:S(2)}) async-start(), calls=%async_computation.15 | async-start | bytes 7864320 | tf_op jit(solution)/shard_map/reduce_scatter | solution.py:378
  956.7 2.2 copy-start.28
  956.7 2.2 copy-start.30
  967.4 436.6 %all-to-all-start.1 = ((bf16[8,48,1024]{2,1,0:T(8,128)(2,1)}), bf16[8,48,1024]{2,1,0:T(8,128)(2,1)S(1)}, u32[]{:S(2)}, u32[]{:S(2)}) async-start(bf16[8,48,1024]{2,1,0:T(8,128)(2,1)} %bitcast.31), calls=%async_computation.1 | async-start | bytes 1572864 | tf_op jit(solution)/shard_map/all_to_all | solution.py:369
  971.7 423.2 %copy-start.4 = (bf16[8,48,1024]{2,1,0:T(8,128)(2,1)S(1)}, bf16[8,48,1024]{2,1,0:T(8,128)(2,1)}, u32[]{:S(2)}) copy-start(bf16[8,48,1024]{2,1,0:T(8,128)(2,1)} %copy-done.3) | copy-start | bytes 2359300
  971.7 423.2 %copy-start.40 = (f32[4,1,256]{2,1,0:T(1,128)S(1)}, f32[4,1,256]{2,1,0:T(1,128)}, u32[]{:S(2)}) copy-start(f32[4,1,256]{2,1,0:T(1,128)} %copy-done.39) | copy-start | bytes 12292
  971.7 423.2 %copy-start.42 = (f32[384]{0:T(512)S(1)}, f32[384]{0:T(512)}, u32[]{:S(2)}) copy-start(f32[384]{0:T(512)} %copy-done.41) | copy-start | bytes 4612
  971.7 538.4 %all-reduce.11.cloned.1.call-start = ((), (), s32[]{:S(2)}) async-start(), calls=%async_computation.20 | async-start | bytes 12255232 | tf_op jit(solution)/shard_map/psum | solution.py:396
  1394.9 6.0 copy-start.48
  1394.9 6.0 copy-start.44
  1394.9 6.8 copy-start.11
  1394.9 6.8 copy-start.46
  1395.0 6.8 copy-start.50
  1402.3 6.1 copy-start.56
  1402.3 6.1 copy-start.53
  1402.3 7.4 copy-start.57
  1402.3 11.2 copy-start.51
  1404.0 34.8 %all-to-all-start.3 = ((bf16[8,48,1024]{2,1,0:T(8,128)(2,1)}), bf16[8,48,1024]{2,1,0:T(8,128)(2,1)S(1)}, u32[]{:S(2)}, u32[]{:S(2)}) async-start(bf16[8,48,1024]{2,1,0:T(8,128)(2,1)} %bitcast.41), calls=%async_computation.3 | async-start | bytes 1572864 | tf_op jit(solution)/shard_map/all_to_all | solution.py:370
  1510.1 4.6 copy-start.19
  1514.7 2.0 copy-start.21
  1514.7 5.0 copy-start.1
  (13 other events, 17.4 us)
Sparse Core Ops, SparseCore 0:
  9.6 117.5 all-gather.8
  157.2 51.0 all-gather.10
  210.8 45.3 all-gather.12
  257.6 45.0 all-gather.14
  304.1 187.3 all-gather.16
  492.9 98.2 all-gather.18
  824.9 126.0 reduce-scatter.15
  953.9 43.3 reduce-scatter.9
  1000.2 95.4 reduce-scatter.13
  1097.9 182.7 reduce-scatter.11
  1283.0 111.8 reduce-scatter.7
  1398.5 111.5 all-reduce.10
where the time goes:
time: 1540 us; the launch traced here: 1530 us
  waiting for transfers between devices  966 us (63%)
  matrix products  248 us (16%)
  local copies, waits for them, and re-layouts  113 us (7%)
  other arithmetic  112 us (7%)
  blocking collectives  39 us (3%)
  starting transfers between devices  18.9 us (1%)
  between operations  16.8 us (1%)
    reduce_scatter x1, waiting for transfers between devices, per_device(): lax.psum_scatter(grad_in_mlp.astype(jnp.bfloat16), 'fsdp', scatter_dimens...  185 us
    all_gather x1, waiting for transfers between devices, per_device(): lax.all_gather(geglu_in, 'fsdp', axis=0, tiled=True)  151 us
    reduce_scatter x1, waiting for transfers between devices, per_device(): lax.psum_scatter(grad_qkv_full.astype(jnp.bfloat16), 'fsdp', scatter_dime...  114 us
    unnamed x13, waiting for transfers between devices  104 us
    reduce_scatter x1, waiting for transfers between devices, per_device(): lax.psum_scatter(grad_out_mlp.astype(jnp.bfloat16), 'fsdp', scatter_dimen...  98.4 us
    all_gather x1, waiting for transfers between devices, per_device(): lax.all_gather(qkv_weight, 'fsdp', axis=0, tiled=True)  96.4 us
    all_gather x1, waiting for transfers between devices, per_device(): lax.all_gather(geglu_out, 'fsdp', axis=0, tiled=True)  88.5 us
    psum x1, waiting for transfers between devices, per_device(): lax.psum(shard_qkv.astype(jnp.bfloat16), 'ctx').astype(jnp.float32)  69.4 us
  transfers between devices with their start and end apart: 16, of which 11 were waited for; matrix products, arithmetic and copies ran while one was open for 13% of the time, Pallas kernels for 0%

commit v1 on v0

v1 whole, which is shorter than its diff:
```python
import functools
import math
import jax
import jax.numpy as jnp
from jax import lax
from jax.experimental import pallas as pl
from jax.experimental.pallas import tpu as pltpu
from jax.sharding import PartitionSpec as P

HEAD_WIDTH = 64
norm_eps = 1e-05
masked_score = -1e30


def head_stack(rows_in, head_count):
    if head_count == 1:
        return rows_in
    lane_head = lax.broadcasted_iota(jnp.int32, rows_in.shape, 1) // HEAD_WIDTH
    zero = jnp.zeros_like(rows_in)
    return jnp.concatenate(
        [jnp.where(lane_head == h, rows_in, zero) for h in range(head_count)], axis=0
    )


def head_pick(stacked_t, head_count, block):
    return jnp.concatenate(
        [
            stacked_t[h * HEAD_WIDTH : (h + 1) * HEAD_WIDTH, h * block : (h + 1) * block]
            for h in range(head_count)
        ],
        axis=0,
    ).T


NT = (((1,), (1,)), ((), ()))


def forward_kernel(
    head_count, block_q, block_k, low_ref, high_ref, begin_ref, end_ref, qkv_ref, out_ref, log_ref, turned_ref
):
    width = out_ref.shape[1]
    step = pl.program_id(0)

    @pl.when(step == 0)
    def prepare():
        turned_ref[...] = qkv_ref[:, 2 * width :].astype(jnp.float32).T.astype(jnp.bfloat16)

    rows = pl.ds(pl.multiple_of(step * block_q, block_q), block_q)
    scale = 1.0 / math.sqrt(HEAD_WIDTH)
    stacked = head_stack(qkv_ref[rows, :width] * jnp.asarray(scale, jnp.bfloat16), head_count)
    begin = jnp.concatenate([begin_ref[:, rows]] * head_count, axis=1)
    end = jnp.concatenate([end_ref[:, rows]] * head_count, axis=1)

    def body(index, carried):
        top, total, acc = carried
        first = pl.multiple_of(index * block_k, block_k)
        keys = qkv_ref[pl.ds(first, block_k), width : 2 * width]
        scores = lax.dot_general(keys, stacked, NT, preferred_element_type=jnp.float32)
        place = first + lax.broadcasted_iota(jnp.int32, scores.shape, 0)
        scores = jnp.where((place >= begin) & (place < end), scores, masked_score)
        new_top = jnp.maximum(top, jnp.max(scores, axis=0, keepdims=True))
        fresh = jnp.exp(scores - new_top)
        fade = jnp.exp(top - new_top)
        total = total * fade + jnp.sum(fresh, axis=0, keepdims=True)
        acc = acc * fade + jnp.dot(
            turned_ref[:, pl.ds(first, block_k)],
            fresh.astype(jnp.bfloat16),
            preferred_element_type=jnp.float32,
        )
        return (new_top, total, acc)

    lanes = head_count * block_q
    top, total, acc = lax.fori_loop(
        low_ref[step],
        high_ref[step],
        body,
        (
            jnp.full((1, lanes), masked_score, jnp.float32),
            jnp.zeros((1, lanes), jnp.float32),
            jnp.zeros((width, lanes), jnp.float32),
        ),
    )
    valid = end > begin
    safe = jnp.where(valid, total, 1.0)
    acc = jnp.where(valid, acc / safe, 0.0)
    log_total = jnp.where(valid, top + jnp.log(safe), 0.0)
    out_ref[...] = head_pick(acc, head_count, block_q)
    log_ref[0] = log_total


def attention_forward(qkv, begin, end, low, high, head_count, block_q, block_k):
    tokens = qkv.shape[0]
    width = head_count * HEAD_WIDTH
    steps = tokens // block_q
    whole = lambda shape: pl.BlockSpec(shape, lambda i, *_: (0,) * len(shape))
    pairs = tokens * tokens // 4 * head_count
    return pl.pallas_call(
        functools.partial(forward_kernel, head_count, block_q, block_k),
        out_shape=(
            jax.ShapeDtypeStruct((tokens, width), jnp.float32),
            jax.ShapeDtypeStruct((steps, 1, head_count * block_q), jnp.float32),
        ),
        grid_spec=pltpu.PrefetchScalarGridSpec(
            num_scalar_prefetch=2,
            grid=(steps,),
            in_specs=[whole((1, tokens)), whole((1, tokens)), whole((tokens, 3 * width))],
            out_specs=(
                pl.BlockSpec((block_q, width), lambda i, *_: (i, 0)),
                pl.BlockSpec((1, 1, head_count * block_q), lambda i, *_: (i, 0, 0)),
            ),
            scratch_shapes=[pltpu.VMEM((width, tokens), jnp.bfloat16)],
        ),
        cost_estimate=pl.CostEstimate(
            flops=pairs * 512, bytes_accessed=tokens * width * 12, transcendentals=pairs
        ),
        name="attention_forward",
    )(low, high, begin, end, qkv)


def turn_back(grads, cosine, sine, head_count):
    half = HEAD_WIDTH // 2
    pieces = []
    for h in range(head_count):
        base = h * HEAD_WIDTH
        pieces += [grads[:, base + half : base + HEAD_WIDTH], grads[:, base : base + half]]
    return grads * cosine + jnp.concatenate(pieces, axis=1) * sine


def backward_kernel(
    head_count,
    block_q,
    block_k,
    low_ref,
    high_ref,
    begin_ref,
    end_ref,
    qkv_ref,
    attended_ref,
    grad_ref,
    log_ref,
    cosine_ref,
    sine_ref,
    out_ref,
    turned_ref,
    key_acc,
    value_acc,
):
    width = attended_ref.shape[1]
    step = pl.program_id(0)

    @pl.when(step == 0)
    def prepare():
        turned_ref[...] = qkv_ref[:, width : 2 * width].astype(jnp.float32).T.astype(jnp.bfloat16)
        key_acc[...] = jnp.zeros_like(key_acc)
        value_acc[...] = jnp.zeros_like(value_acc)

    rows = pl.ds(pl.multiple_of(step * block_q, block_q), block_q)
    scale = 1.0 / math.sqrt(HEAD_WIDTH)
    stacked = head_stack(qkv_ref[rows, :width] * jnp.asarray(scale, jnp.bfloat16), head_count)
    grads = grad_ref[rows, :]
    grad_stacked = head_stack(grads, head_count)
    begin = jnp.concatenate([begin_ref[:, rows]] * head_count, axis=1)
    end = jnp.concatenate([end_ref[:, rows]] * head_count, axis=1)
    product = (grads.astype(jnp.float32) * attended_ref[rows, :]).T
    delta = jnp.concatenate(
        [
            jnp.sum(product[h * HEAD_WIDTH : (h + 1) * HEAD_WIDTH], axis=0, keepdims=True)
            for h in range(head_count)
        ],
        axis=1,
    )
    log_total = log_ref[0]

    def body(index, acc):
        first = pl.multiple_of(index * block_k, block_k)
        span = pl.ds(first, block_k)
        keys = qkv_ref[span, width : 2 * width]
        values = qkv_ref[span, 2 * width :]
        scores = lax.dot_general(keys, stacked, NT, preferred_element_type=jnp.float32)
        grad_probs = lax.dot_general(values, grad_stacked, NT, preferred_element_type=jnp.float32)
        place = first + lax.broadcasted_iota(jnp.int32, scores.shape, 0)
        scores = jnp.where((place >= begin) & (place < end), scores, masked_score)
        probs = jnp.exp(scores - log_total)
        grad_scores = (probs * (grad_probs - delta)).astype(jnp.bfloat16)
        value_acc[span, :] += jnp.dot(
            probs.astype(jnp.bfloat16), grad_stacked, preferred_element_type=jnp.float32
        )
        key_acc[span, :] += jnp.dot(grad_scores, stacked, preferred_element_type=jnp.float32)
        return acc + jnp.dot(
            turned_ref[:, span], grad_scores, preferred_element_type=jnp.float32
        )

    acc = lax.fori_loop(
        low_ref[step],
        high_ref[step],
        body,
        jnp.zeros((width, head_count * block_q), jnp.float32),
    )
    grad_queries = head_pick(acc, head_count, block_q) * scale
    out_ref[rows, :width] = turn_back(
        grad_queries, cosine_ref[rows, :], sine_ref[rows, :], head_count
    ).astype(jnp.bfloat16)

    @pl.when(step == pl.num_programs(0) - 1)
    def finish():
        @pl.loop(0, pl.num_programs(0))
        def each(index):
            span = pl.ds(pl.multiple_of(index * block_q, block_q), block_q)
            out_ref[span, width : 2 * width] = turn_back(
                key_acc[span, :], cosine_ref[span, :], sine_ref[span, :], head_count
            ).astype(jnp.bfloat16)
            out_ref[span, 2 * width :] = value_acc[span, :].astype(jnp.bfloat16)


def attention_backward(
    qkv, attended, grads, log_total, begin, end, low, high, cosine, sine, head_count, block_q, block_k
):
    tokens = qkv.shape[0]
    width = head_count * HEAD_WIDTH
    steps = tokens // block_q
    whole = lambda shape: pl.BlockSpec(shape, lambda i, *_: (0,) * len(shape))
    pairs = tokens * tokens // 4 * head_count
    return pl.pallas_call(
        functools.partial(backward_kernel, head_count, block_q, block_k),
        out_shape=jax.ShapeDtypeStruct((tokens, 3 * width), jnp.bfloat16),
        grid_spec=pltpu.PrefetchScalarGridSpec(
            num_scalar_prefetch=2,
            grid=(steps,),
            in_specs=[
                whole((1, tokens)),
                whole((1, tokens)),
                whole((tokens, 3 * width)),
                whole((tokens, width)),
                whole((tokens, width)),
                pl.BlockSpec((1, 1, head_count * block_q), lambda i, *_: (i, 0, 0)),
                whole((tokens, width)),
                whole((tokens, width)),
            ],
            out_specs=whole((tokens, 3 * width)),
            scratch_shapes=[
                pltpu.VMEM((width, tokens), jnp.bfloat16),
                pltpu.VMEM((tokens, width), jnp.float32),
                pltpu.VMEM((tokens, width), jnp.float32),
            ],
        ),
        cost_estimate=pl.CostEstimate(
            flops=pairs * 1280, bytes_accessed=tokens * width * 30, transcendentals=pairs
        ),
        name="attention_backward",
    )(low, high, begin, end, qkv, attended, grads, log_total, cosine, sine)


def spans(places, lengths_row):
    ends = jnp.cumsum(lengths_row)
    past = (places[:, None] >= ends[None, :]).astype(jnp.int32)
    begin = jnp.sum(past * lengths_row[None, :], axis=1)
    before = (places[:, None] >= (ends - lengths_row)[None, :]).astype(jnp.int32)
    end = jnp.sum(before * lengths_row[None, :], axis=1)
    valid = places < ends[-1]
    return (jnp.where(valid, begin, 0), jnp.where(valid, end, 0), places - begin, valid)


def key_range(begin, end, block_q, block_k):
    begin_blocks = jnp.where(end > begin, begin, jnp.int32(1 << 30)).reshape(-1, block_q)
    high = (jnp.max(end.reshape(-1, block_q), axis=1) + block_k - 1) // block_k
    low = jnp.minimum(jnp.min(begin_blocks, axis=1) // block_k, high)
    return (low, high)


def rotary_tables(offset, head_count):
    half = HEAD_WIDTH // 2
    inverse = 160000.0 ** (-2.0 * jnp.arange(half, dtype=jnp.float32) / HEAD_WIDTH)
    angles = offset.astype(jnp.float32)[:, None] * inverse[None, :]
    cosine, sine = (jnp.cos(angles), jnp.sin(angles))
    return (
        jnp.concatenate([cosine, cosine] * head_count, axis=1),
        jnp.concatenate([sine, -sine] * head_count, axis=1),
    )


def layer_norm(rows_in, gain_vec):
    row_mean = jnp.mean(rows_in, axis=-1, keepdims=True)
    centred = rows_in - row_mean
    variance = jnp.mean(centred * centred, axis=-1, keepdims=True)
    return centred * lax.rsqrt(variance + norm_eps) * gain_vec


def rotate(projected, cosine, sine):
    row_count, width = projected.shape
    half_width = HEAD_WIDTH // 2
    by_head = projected.reshape(row_count, width // HEAD_WIDTH, HEAD_WIDTH)
    turned = jnp.concatenate([by_head[..., half_width:], by_head[..., :half_width]], axis=-1)
    return (by_head * cosine[:, None, :] - turned * sine[:, None, :]).reshape(row_count, width)


def swap(value, axis, bit):
    pairs = [(i, i ^ bit) for i in range(lax.axis_size(axis))]
    return lax.ppermute(value, axis, pairs)


def bit_of(axis, bit):
    return (lax.axis_index(axis) // bit) % 2 == 1


def bits_below(count):
    return [1 << i for i in range(count.bit_length() - 1)]


def reduce_pieces(pieces, labels, order):
    labels = list(labels)
    for axis, bit in order:
        at = labels.index((axis, bit))
        labels.pop(at)
        first = lax.index_in_dim(pieces, 0, at, keepdims=False)
        second = lax.index_in_dim(pieces, 1, at, keepdims=False)
        upper = bit_of(axis, bit)
        arrived = swap(jnp.where(upper, first, second), axis, bit)
        kept = jnp.where(upper, second, first)
        pieces = (kept.astype(jnp.float32) + arrived.astype(jnp.float32)).astype(jnp.bfloat16)
    return pieces


def gather_pieces(piece, labels, order):
    held = []
    for axis, bit in reversed(order):
        arrived = swap(piece, axis, bit)
        upper = bit_of(axis, bit)
        held = [label for label in labels if label in held or label == (axis, bit)]
        piece = jnp.stack(
            [jnp.where(upper, arrived, piece), jnp.where(upper, piece, arrived)],
            axis=held.index((axis, bit)),
        )
    return piece


def keep_and_send(first, second):
    upper = bit_of("ctx", 1)
    return (jnp.where(upper, second, first), jnp.where(upper, first, second))


def core_product(left, first, second):
    kept, sent = keep_and_send(first, second)
    left_all = jnp.concatenate([left, swap(left, "ctx", 1)], axis=0)
    right_all = jnp.concatenate([kept, swap(sent, "ctx", 1)], axis=0)
    return lax.dot_general(
        left_all, right_all, (((0,), (0,)), ((), ())), preferred_element_type=jnp.float32
    ).astype(jnp.bfloat16)


def shard_sum(product, by_columns):
    shards = lax.axis_size("fsdp")
    slices = lax.axis_size("ctx") // 2
    rows, columns = product.shape
    shard_labels = [("fsdp", bit) for bit in reversed(bits_below(shards))]
    slice_labels = [("ctx", 2 * bit) for bit in reversed(bits_below(slices))]
    if by_columns:
        cut = product.reshape(shards, rows // shards, slices, columns // slices)
        cut = jnp.transpose(cut, (0, 2, 1, 3))
    else:
        cut = product.reshape(shards, slices, rows // shards // slices, columns)
    parts = []
    half = cut.shape[2] // 2
    tail = list(reversed(shard_labels))
    for lead, orders in (
        (cut[:, :, :half], list(reversed(slice_labels))),
        (cut[:, :, half:], slice_labels),
    ):
        pieces = lead.reshape((2,) * (len(shard_labels) + len(slice_labels)) + lead.shape[2:])
        piece = reduce_pieces(pieces, shard_labels + slice_labels, orders + tail)
        whole = gather_pieces(piece, slice_labels, orders)
        parts.append(whole.reshape((slices,) + piece.shape))
    both = jnp.concatenate(parts, axis=1)
    if by_columns:
        return jnp.transpose(both, (1, 0, 2)).reshape(rows // shards, columns)
    return both.reshape(rows // shards, columns)


def join_cores(own):
    other = swap(own, "ctx", 1)
    upper = bit_of("ctx", 1)
    return jnp.concatenate(
        [jnp.where(upper, other, own), jnp.where(upper, own, other)], axis=1
    ).astype(jnp.float32)


def sum_over(value, axes):
    for axis in axes:
        for bit in bits_below(lax.axis_size(axis)):
            value = value + swap(value, axis, bit)
    return value


def own_shard(vector):
    width = vector.shape[0] // lax.axis_size("fsdp")
    return lax.dynamic_slice_in_dim(vector, lax.axis_index("fsdp") * width, width, 0)


def per_device(
    inputs,
    cotangent,
    lengths,
    piece_route,
    gain_one,
    qkv_weight,
    attn_out,
    gain_two,
    geglu_in,
    geglu_out,
):
    ctx_count = lax.axis_size("ctx")
    own_index = lax.axis_index("ctx")
    row_count = inputs.shape[1]
    model_width = inputs.shape[2]
    piece_rows = row_count // ctx_count
    tokens = row_count * ctx_count
    own_heads = model_width // HEAD_WIDTH // ctx_count
    own_width = own_heads * HEAD_WIDTH
    block_q = math.gcd(tokens, 256)
    block_k = math.gcd(tokens, 512)
    lengths_row = lengths[0]
    own_route = piece_route[0, 0]
    slot_ids = jnp.arange(ctx_count, dtype=jnp.int32)
    outgoing = jnp.sum(
        slot_ids[None, :] * (own_route[None, :] == slot_ids[:, None]).astype(jnp.int32), axis=1
    )

    def exchange(blocks):
        return lax.all_to_all(blocks, "ctx", split_axis=0, concat_axis=0, tiled=True)

    def to_slots(rows_in):
        return jnp.take(rows_in.reshape(ctx_count, piece_rows, model_width), outgoing, axis=0)

    def to_heads(rows_in):
        by_heads = rows_in.reshape(row_count, ctx_count, -1)
        return exchange(jnp.transpose(by_heads, (1, 0, 2))).reshape(tokens, -1)

    def to_rows(heads_in):
        return exchange(heads_in.reshape(ctx_count, row_count, -1))

    arrived = exchange(to_slots(inputs[0]))
    grad_arrived = exchange(to_slots(cotangent[0]))
    residual = arrived.reshape(row_count, model_width).astype(jnp.float32)
    places = own_index * row_count + jnp.arange(row_count, dtype=jnp.int32)
    unused_begin, unused_end, offset, is_valid = spans(places, lengths_row)
    pack_begin, pack_end, pack_offset, unused_valid = spans(
        jnp.arange(tokens, dtype=jnp.int32), lengths_row
    )
    grad_final = jnp.where(
        is_valid[:, None], grad_arrived.reshape(row_count, model_width).astype(jnp.float32), 0.0
    )
    gain_attn_low, qkv_full, attn_full = (
        lax.all_gather(gain_one, "fsdp", axis=0, tiled=True),
        lax.all_gather(qkv_weight, "fsdp", axis=0, tiled=True),
        lax.all_gather(attn_out, "fsdp", axis=0, tiled=True),
    )
    gain_mlp_low, in_full, out_full = (
        lax.all_gather(gain_two, "fsdp", axis=0, tiled=True),
        lax.all_gather(geglu_in, "fsdp", axis=0, tiled=True),
        lax.all_gather(geglu_out, "fsdp", axis=0, tiled=True),
    )
    gain_attn = gain_attn_low.astype(jnp.float32)
    act_attn = layer_norm(residual, gain_attn).astype(jnp.bfloat16)
    projected = jnp.dot(act_attn, qkv_full, preferred_element_type=jnp.float32)
    cosine, sine = rotary_tables(offset, 1)
    queries, keys = (
        rotate(projected[:, :model_width], cosine, sine).astype(jnp.bfloat16),
        rotate(projected[:, model_width : 2 * model_width], cosine, sine).astype(jnp.bfloat16),
    )
    values = projected[:, 2 * model_width :].astype(jnp.bfloat16)
    joined = jnp.stack(
        [part.reshape(row_count, ctx_count, own_width) for part in (queries, keys, values)], axis=2
    )
    qkv_heads = to_heads(joined.reshape(row_count, -1))
    low, high = key_range(pack_begin, pack_end, block_q, block_k)
    pack_begin, pack_end = (pack_begin[None, :], pack_end[None, :])
    attended_heads, log_total = attention_forward(
        qkv_heads, pack_begin, pack_end, low, high, own_heads, block_q, block_k
    )
    attn_low = jnp.transpose(to_rows(attended_heads.astype(jnp.bfloat16)), (1, 0, 2)).reshape(
        row_count, model_width
    )
    branch_attn = jnp.dot(attn_low, attn_full, preferred_element_type=jnp.float32)
    middle = residual + branch_attn
    gain_mlp = gain_mlp_low.astype(jnp.float32)
    act_mlp = layer_norm(middle, gain_mlp).astype(jnp.bfloat16)
    up_both = jnp.dot(act_mlp, in_full, preferred_element_type=jnp.float32)
    ff_width = up_both.shape[1] // 2
    hidden = (jax.nn.gelu(up_both[:, :ff_width], approximate=False) * up_both[:, ff_width:]).astype(
        jnp.bfloat16
    )
    branch_mlp = jnp.dot(hidden, out_full, preferred_element_type=jnp.float32)
    final_rows = jnp.where(is_valid[:, None], middle + branch_mlp, 0.0)
    square_sums = jnp.stack(
        [
            jnp.sum(final_rows * final_rows),
            jnp.sum(jnp.where(is_valid[:, None], branch_attn * branch_attn, 0.0)),
            jnp.sum(jnp.where(is_valid[:, None], branch_mlp * branch_mlp, 0.0)),
        ]
    )
    out_slots = final_rows.astype(jnp.bfloat16).reshape(ctx_count, piece_rows, model_width)
    back_out = exchange(out_slots)
    block_out = jnp.take(back_out, own_route, axis=0).reshape(1, row_count, model_width)
    grad_mlp_low = grad_final.astype(jnp.bfloat16)
    half_width = model_width // 2
    grad_out_mlp = core_product(hidden, grad_mlp_low[:, :half_width], grad_mlp_low[:, half_width:])
    grad_hidden = lax.dot_general(
        grad_mlp_low, out_full, NT, preferred_element_type=jnp.float32
    )

    def gated(leading, trailing):
        return jax.nn.gelu(leading, approximate=False) * trailing

    unused_gate, gate_back = jax.vjp(gated, up_both[:, :ff_width], up_both[:, ff_width:])
    grad_leading, grad_trailing = gate_back(grad_hidden)
    grad_leading, grad_trailing = (
        grad_leading.astype(jnp.bfloat16),
        grad_trailing.astype(jnp.bfloat16),
    )
    grad_up = jnp.concatenate([grad_leading, grad_trailing], axis=1)
    grad_in_mlp = core_product(act_mlp, grad_leading, grad_trailing)
    grad_act_mlp = lax.dot_general(grad_up, in_full, NT, preferred_element_type=jnp.float32)
    unused_norm, norm_back_mlp = jax.vjp(layer_norm, middle, gain_mlp)
    grad_middle_norm, grad_gain_mlp = norm_back_mlp(grad_act_mlp)
    grad_middle = grad_final + grad_middle_norm
    grad_attn_low = grad_middle.astype(jnp.bfloat16)
    grad_attn_proj = core_product(
        attn_low, grad_attn_low[:, :half_width], grad_attn_low[:, half_width:]
    )
    grad_attended = lax.dot_general(
        grad_attn_low, attn_full, NT, preferred_element_type=jnp.float32
    ).astype(jnp.bfloat16)
    pack_cosine, pack_sine = rotary_tables(pack_offset, own_heads)
    block_back = math.gcd(tokens, 256)
    low_back, high_back = key_range(pack_begin[0], pack_end[0], block_q, block_back)
    grad_heads = attention_backward(
        qkv_heads,
        attended_heads,
        to_heads(grad_attended),
        log_total,
        pack_begin,
        pack_end,
        low_back,
        high_back,
        pack_cosine,
        pack_sine,
        own_heads,
        block_q,
        block_back,
    )
    grad_projected = jnp.transpose(
        to_rows(grad_heads).reshape(ctx_count, row_count, 3, own_width), (1, 2, 0, 3)
    ).reshape(row_count, 3 * model_width)
    half_three = 3 * model_width // 2
    grad_qkv = core_product(
        act_attn, grad_projected[:, :half_three], grad_projected[:, half_three:]
    )
    grad_act_attn = lax.dot_general(
        grad_projected, qkv_full, NT, preferred_element_type=jnp.float32
    )
    unused_first, norm_back_attn = jax.vjp(layer_norm, residual, gain_attn)
    grad_resid_norm, grad_gain_attn = norm_back_attn(grad_act_attn)
    grad_residual = (grad_middle + grad_resid_norm).astype(jnp.bfloat16)
    back_grad = exchange(grad_residual.reshape(ctx_count, piece_rows, model_width))
    grad_inputs = jnp.take(back_grad, own_route, axis=0).reshape(1, row_count, model_width)
    total_out = join_cores(shard_sum(grad_out_mlp, True))
    total_in = join_cores(shard_sum(grad_in_mlp, False))
    total_attn = join_cores(shard_sum(grad_attn_proj, False))
    total_qkv = join_cores(shard_sum(grad_qkv, False))
    total_gain_one = own_shard(sum_over(grad_gain_attn, ("ctx", "fsdp")))
    total_gain_two = own_shard(sum_over(grad_gain_mlp, ("ctx", "fsdp")))
    total_squares = sum_over(square_sums, ("ctx",))
    valid_count = jnp.sum(lengths_row).astype(jnp.float32)
    rms_stats = jnp.sqrt(total_squares / (valid_count * model_width))[None, :]
    return (
        block_out,
        grad_inputs,
        total_gain_one,
        total_qkv,
        total_attn,
        total_gain_two,
        total_in,
        total_out,
        rms_stats,
    )


def solution(mesh):
    placed = (
        P("fsdp", "ctx", None),
        P("fsdp", "ctx", None),
        P("fsdp", None),
        P("fsdp", "ctx", None),
        P("fsdp"),
        P("fsdp", None),
        P("fsdp", None),
        P("fsdp"),
        P("fsdp", None),
        P("fsdp", None),
    )
    return jax.shard_map(
        per_device,
        mesh=mesh,
        in_specs=placed,
        out_specs=(
            P("fsdp", "ctx", None),
            P("fsdp", "ctx", None),
            P("fsdp"),
            P("fsdp", None),
            P("fsdp", None),
            P("fsdp"),
            P("fsdp", None),
            P("fsdp", None),
            P("fsdp", None),
        ),
        check_vma=False,
    )
```

time: 1540 us -> 984 us (0.64)
  waiting for transfers between devices: 966 us -> 473 us
  matrix products: 248 us -> 92.1 us
  starting transfers between devices: 18.9 us -> 124 us
  Pallas kernels: 0 us -> 73.6 us
  other arithmetic: 112 us -> 86.5 us
  blocking collectives: 39 us -> 16.1 us
  local copies, waits for them, and re-layouts: 113 us -> 96.7 us
    reduce_scatter x4 -> x0, waiting for transfers between devices: 423 us -> none  [the longest x1 185 us: per_device(): lax.psum_scatter(grad_in_mlp.astype(jnp.bfloat16), 'fsdp', scatter_dimens...]
    ppermute x0 -> x73, waiting for transfers between devices: none -> 182 us  [swap(): return lax.ppermute(value, axis, pairs)]
    dot_general x36 -> x8, matrix products: 221 us -> 61.4 us  [the longest x4 22.4 us: core_product(): lax.dot_general(left_all, right_all, (((0,), (0,)), ((), ())), preferred_...]
    unnamed x13 -> x4, waiting for transfers between devices: 104 us -> 2.61 us
    pallas_call x0 -> x2, Pallas kernels: none -> 73.6 us  [the longest x1 43.5 us: attention_backward(): pl.pallas_call(functools.partial(backward_kernel, head_count, block_q, bl...]
    psum x1 -> x0, waiting for transfers between devices: 69.4 us -> none  [per_device(): lax.psum(shard_qkv.astype(jnp.bfloat16), 'ctx').astype(jnp.float32)]
    ppermute x0 -> x73, starting transfers between devices: none -> 67.1 us  [swap(): return lax.ppermute(value, axis, pairs)]
    all_gather x1, waiting for transfers between devices: 151 us -> 86.2 us  [per_device(): lax.all_gather(geglu_in, 'fsdp', axis=0, tiled=True)]
  transfers between devices with their start and end apart: 16 -> 85, of which waited for: 11 -> 46; matrix products, arithmetic and copies ran while one was open for 13% -> 27% of each run, Pallas kernels for 0% -> 8%
where the time goes in v1:
time: 984 us; the launch traced here: 978 us
  waiting for transfers between devices  473 us (48%)
  starting transfers between devices  124 us (13%)
  local copies, waits for them, and re-layouts  96.7 us (10%)
  matrix products  92.1 us (9%)
  other arithmetic  86.5 us (9%)
  Pallas kernels  73.6 us (7%)
  between operations  16.2 us (2%)
  blocking collectives  16.1 us (2%)
    ppermute x73, waiting for transfers between devices, swap(): return lax.ppermute(value, axis, pairs)  182 us
    all_gather x1, waiting for transfers between devices, per_device(): lax.all_gather(qkv_weight, 'fsdp', axis=0, tiled=True)  93.1 us
    all_gather x1, waiting for transfers between devices, per_device(): lax.all_gather(geglu_out, 'fsdp', axis=0, tiled=True)  87.8 us
    all_gather x1, waiting for transfers between devices, per_device(): lax.all_gather(geglu_in, 'fsdp', axis=0, tiled=True)  86.2 us
    ppermute x73, starting transfers between devices, swap(): return lax.ppermute(value, axis, pairs)  67.1 us
    all_to_all x8, starting transfers between devices, exchange(): lax.all_to_all(blocks, 'ctx', split_axis=0, concat_axis=0, tiled=True)  56.6 us
    pallas_call x1, Pallas kernels, attention_backward(): pl.pallas_call(functools.partial(backward_kernel, head_count, block_q, bl...  43.5 us
    pallas_call x1, Pallas kernels, attention_forward(): pl.pallas_call(functools.partial(forward_kernel, head_count, block_q, blo...  30.2 us
  transfers between devices with their start and end apart: 85, of which 46 were waited for; matrix products, arithmetic and copies ran while one was open for 27% of the time, Pallas kernels for 8%

profile of v1, /device:TPU:1, one launch (start us, length us, event | category | flops | bytes accessed | tf_op | source)
XLA Modules:
  0.0 978.3 jit_solution(3212225499875288126)
XLA Ops:
  12.2 5.3 all-to-all-start
  18.1 9.5 all-gather
  34.1 93.1 %all-gather.7.cloned.1.call-done = bf16[1024,3072]{1,0:T(8,128)(2,1)} async-done(((bf16[256,3072]{1,0:T(8,128)(2,1)}), bf16[1024,3072]{1,0:T(8,128)(2,1)}) %all-gather.7.cloned.1.call-update) | async-done | bytes 6291472 | tf_op jit(solution)/shard_map/all_gather | solution.py:453
  127.2 7.8 fusion.137
  136.9 4.0 fusion.125
  157.0 3.8 fusion.56
  163.5 4.7 all-to-all-start.1
  172.0 7.1 multiply_sine_fusion
  179.1 15.1 %all-to-all-done.1 = bf16[8,384,384]{2,1,0:T(8,128)(2,1)} async-done(((bf16[8,384,384]{2,1,0:T(8,128)(2,1)}), bf16[8,384,384]{2,1,0:T(8,128)(2,1)}, u32[]{:S(2)}, u32[]{:S(2)}) %all-to-all-start.1) | async-done | bytes 2359328 | tf_op jit(solution)/shard_map/all_to_all | solution.py:428
  194.1 7.1 all-to-all-start.4
  202.0 6.6 all-gather.1
  209.3 8.5 pad_maximum_fusion
  217.8 30.2 %attention_forward.1 = (f32[3072,128]{1,0:T(8,128)}, f32[12,1,512]{2,1,0:T(1,128)}) custom-call(s32[12]{0:T(128)} %get-tuple-element.147.low_ref, s32[12]{0:T(128)} %get-tuple-element.148.high_ref, s32[1,3072]{1,0:T(1,128)} %get-tuple-element.159.begin_ref, s32[1,3072]{1,0:T(1,128)} %get-tuple-element.158.end_ref, bf16[3072,384]{1,0:T(8,128)(2,1)} %bitcast.22.qkv_ref), custom_call_target="tpu_custom_call" | custom-call | flops 2415919104 | bytes 4718592 | tf_op jit(solution)/shard_map/attention_forward/pallas_call | solution.py:97
  250.7 6.3 all-to-all-start.2
  260.0 6.1 all-to-all-done.2
  266.0 3.6 collective-permute-start.20
  269.6 4.0 fusion.123
  275.1 86.2 %all-gather.11.cloned.1.call-done = bf16[1024,5248]{1,0:T(8,128)(2,1)} async-done(((bf16[256,5248]{1,0:T(8,128)(2,1)}), bf16[1024,5248]{1,0:T(8,128)(2,1)}) %all-gather.11.cloned.1.call-update) | async-done | bytes 10747920 | tf_op jit(solution)/shard_map/all_gather | solution.py:458
  361.3 11.9 %fusion.138 = f32[384,5248]{1,0:T(8,128)} fusion(bf16[384,1024]{1,0:T(8,128)(2,1)} %multiply_convert_fusion.2, bf16[1024,5248]{1,0:T(8,128)(2,1)} %all-gather.11.cloned.1.call-done), kind=kOutput, calls=%fused_computation.386 | convolution fusion | flops 4127195136 | bytes 19595264 | tf_op jit(solution)/shard_map/dot_general | solution.py:486
  373.2 87.8 %all-gather.13.cloned.1.call-done = bf16[2624,1024]{1,0:T(8,128)(2,1)} async-done(((bf16[656,1024]{1,0:T(8,128)(2,1)}), bf16[2624,1024]{1,0:T(8,128)(2,1)}) %all-gather.13.cloned.1.call-update) | async-done | bytes 5373968 | tf_op jit(solution)/shard_map/all_gather | solution.py:459
  461.0 16.1 %broadcast_select_fusion.1 = (bf16[384,2624]{1,0:T(8,128)(2,1)}, bf16[384,2624]{1,0:T(8,128)(2,1)S(1)}, bf16[384,2624]{1,0:T(8,128)(2,1)S(1)}, f32[384,2624]{1,0:T(8,128)S(1)}) fusion(pred[]{:T(512)S(6)} %eq.142, f32[384,5248]{1,0:T(8,128)} %fusion.138, bf16[384,1024]{1,0:T(8,128)(2,1)} %copy-done.20, bf16[2624,1024]{1,0:T(8,128)(2,1)} %all-gather.13.cloned.1.call-done), kind=kOutput, calls=%fused_computation.52 | convolution fusion | flops 2141184000 | bytes 24297472 | tf_op jit(solution)/shard_map/dot_general | solution.py:506
  480.3 16.7 %fusion.12 = f32[384,1024]{1,0:T(8,128)S(1)} fusion(bf16[1024,5248]{1,0:T(8,128)(2,1)} %all-gather.11.cloned.1.call-done, bf16[384,2624]{1,0:T(8,128)(2,1)} %copy-done.23, bf16[384,2624]{1,0:T(8,128)(2,1)S(1)} %get-tuple-element.55), kind=kOutput, calls=%fused_computation.30 | convolution fusion | flops 4135256064 | bytes 16351232 | tf_op jit(solution)/shard_map/dot_general | solution.py:521
  497.1 6.9 multiply_reduce_fusion
  508.0 4.1 copy.514
  513.1 4.2 all-to-all-start.5
  521.8 4.0 copy.501
  544.0 5.1 collective-permute-start.40
  553.6 6.1 collective-permute-done.28
  560.0 6.2 collective-permute-done.22
  601.6 16.3 %all-to-all-start.3 = ((bf16[8,48,1024]{2,1,0:T(8,128)(2,1)}), bf16[8,48,1024]{2,1,0:T(8,128)(2,1)S(1)}, u32[]{:S(2)}, u32[]{:S(2)}) async-start(bf16[8,48,1024]{2,1,0:T(8,128)(2,1)} %bitcast.27), calls=%async_computation.3 | async-start | bytes 1572864 | tf_op jit(solution)/shard_map/all_to_all | solution.py:428
  618.1 43.5 %attention_backward.1 = bf16[3072,384]{1,0:T(8,128)(2,1)} custom-call(s32[12]{0:T(128)} %get-tuple-element.60.low_ref, s32[12]{0:T(128)} %get-tuple-element.61.high_ref, s32[1,3072]{1,0:T(1,128)} %get-tuple-element.159.begin_ref, s32[1,3072]{1,0:T(1,128)} %get-tuple-element.158.end_ref, bf16[3072,384]{1,0:T(8,128)(2,1)} %bitcast.22.qkv_ref, ...), custom_call_target="tpu_custom_call" | custom-call | flops 6039797760 | bytes 11796480 | tf_op jit(solution)/shard_map/attention_backward/pallas_call | solution.py:223
  661.6 4.3 copy.469
  665.9 4.8 all-to-all-start.6
  675.1 4.1 copy.502
  679.1 9.5 convolution_convert_fusion
  688.6 7.9 copy.503
  696.6 4.5 fusion.124
  704.6 4.1 copy.515
  708.7 6.0 convolution_convert_fusion.1
  714.7 5.7 reshape.524
  729.7 19.7 %collective-permute-done.63 = bf16[2,2,2,328,128]{4,3,0,1,2:T(8,128)(2,1)S(1)} collective-permute-done((bf16[2,2,2,328,128]{4,3,0,1,2:T(8,128)(2,1)S(1)}, bf16[2,2,2,328,128]{4,3,0,1,2:T(8,128)(2,1)S(1)}, u32[]{:S(2)}, u32[]{:S(2)}) %collective-permute-start.63) | collective-permute-done | bytes 671776 | tf_op jit(solution)/shard_map/ppermute | solution.py:298
  754.2 5.3 fusion.43
  760.4 12.8 %collective-permute-done.57 = bf16[2,2,2,328,128]{4,3,2,1,0:T(8,128)(2,1)} collective-permute-done((bf16[2,2,2,328,128]{4,3,2,1,0:T(8,128)(2,1)}, bf16[2,2,2,328,128]{4,3,2,1,0:T(8,128)(2,1)}, u32[]{:S(2)}, u32[]{:S(2)}) %collective-permute-start.57) | collective-permute-done | bytes 671776 | tf_op jit(solution)/shard_map/ppermute | solution.py:298
  789.6 8.0 all-to-all-start.7
  801.4 14.0 %collective-permute-done.58 = bf16[2,2,328,128]{3,2,1,0:T(8,128)(2,1)S(1)} collective-permute-done((bf16[2,2,328,128]{3,2,1,0:T(8,128)(2,1)}, bf16[2,2,328,128]{3,2,1,0:T(8,128)(2,1)S(1)}, u32[]{:S(2)}, u32[]{:S(2)}) %collective-permute-start.58) | collective-permute-done | bytes 335904 | tf_op jit(solution)/shard_map/ppermute | solution.py:298
  815.7 4.7 collective-permute-done.65
  820.8 3.8 collective-permute-done.59
  824.8 4.9 collective-permute-done.66
  829.7 4.9 collective-permute-done.60
  853.1 4.8 collective-permute-done.62
  859.0 3.5 collective-permute-done.68
  862.7 5.5 collective-permute-start.69
  868.2 4.4 convolution_convert_fusion.2
  881.3 3.9 collective-permute-done.50
  885.5 10.1 %collective-permute-done.44 = bf16[2,32,2624]{2,1,0:T(8,128)(2,1)S(1)} collective-permute-done((bf16[2,32,2624]{2,1,0:T(8,128)(2,1)S(1)}, bf16[2,32,2624]{2,1,0:T(8,128)(2,1)S(1)}, u32[]{:S(2)}, u32[]{:S(2)}) %collective-permute-start.44) | collective-permute-done | bytes 335904 | tf_op jit(solution)/shard_map/ppermute | solution.py:298
  896.7 9.1 collective-permute-done.45
  907.5 3.8 collective-permute-done.46
  914.6 4.0 collective-permute-done.53
  922.9 5.9 collective-permute-start.54
  930.7 4.7 collective-permute-done.9
  936.5 4.2 collective-permute-done.15
  941.2 6.8 collective-permute-done.16
  952.3 3.9 collective-permute-done.12
  963.2 6.0 copy.535
  (462 shorter events, 214.5 us)
Async XLA Ops:
  7.2 120.0 %all-gather.7.cloned.1.call-start = ((), (), s32[]{:S(2)}) async-start(), calls=%async_computation.8 | async-start | bytes 7864320 | tf_op jit(solution)/shard_map/all_gather | solution.py:453
  7.9 261.7 %all-gather.9.cloned.1.call-start = ((), (), s32[]{:S(2)}) async-start(), calls=%async_computation.9 | async-start | bytes 2621440 | tf_op jit(solution)/shard_map/all_gather | solution.py:454
  8.7 352.6 %all-gather.11.cloned.1.call-start = ((), (), s32[]{:S(2)}) async-start(), calls=%async_computation.10 | async-start | bytes 13434880 | tf_op jit(solution)/shard_map/all_gather | solution.py:458
  12.2 20.0 %all-to-all-start = ((bf16[8,48,1024]{2,1,0:T(8,128)(2,1)}), bf16[8,48,1024]{2,1,0:T(8,128)(2,1)S(1)}, u32[]{:S(2)}, u32[]{:S(2)}) async-start(bf16[8,48,1024]{2,1,0:T(8,128)(2,1)} %get-tuple-element.154), calls=%async_computation | async-start | bytes 1572864 | tf_op jit(solution)/shard_map/all_to_all | solution.py:428
  17.5 443.5 %all-gather.13.cloned.1.call-start = ((), (), s32[]{:S(2)}) async-start(), calls=%async_computation.11 | async-start | bytes 6717440 | tf_op jit(solution)/shard_map/all_gather | solution.py:459
  163.5 30.6 %all-to-all-start.1 = ((bf16[8,384,384]{2,1,0:T(8,128)(2,1)}), bf16[8,384,384]{2,1,0:T(8,128)(2,1)}, u32[]{:S(2)}, u32[]{:S(2)}) async-start(bf16[8,384,384]{2,1,0:T(8,128)(2,1)} %copy.463), calls=%async_computation.1 | async-start | bytes 4718592 | tf_op jit(solution)/shard_map/all_to_all | solution.py:428
  194.1 56.5 %all-to-all-start.4 = ((bf16[8,48,1024]{2,1,0:T(8,128)(2,1)}), bf16[8,48,1024]{2,1,0:T(8,128)(2,1)S(1)}, u32[]{:S(2)}, u32[]{:S(2)}) async-start(bf16[8,48,1024]{2,1,0:T(8,128)(2,1)} %get-tuple-element.153), calls=%async_computation.4 | async-start | bytes 1572864 | tf_op jit(solution)/shard_map/all_to_all | solution.py:428
  250.7 15.4 %all-to-all-start.2 = ((bf16[8,384,128]{1,2,0:T(8,128)(2,1)}), bf16[8,384,128]{1,2,0:T(8,128)(2,1)}, u32[]{:S(2)}, u32[]{:S(2)}) async-start(bf16[8,384,128]{1,2,0:T(8,128)(2,1)} %copy.464), calls=%async_computation.2 | async-start | bytes 1572864 | tf_op jit(solution)/shard_map/all_to_all | solution.py:428
  257.5 610.6 %collective-permute-start.5 = (bf16[384,1024]{1,0:T(8,128)(2,1)}, bf16[384,1024]{1,0:T(8,128)(2,1)}, u32[]{:S(2)}, u32[]{:S(2)}) collective-permute-start(bf16[384,1024]{1,0:T(8,128)(2,1)} %fusion.41), channel_id=1, source_target_pairs={{0,4},{4,0},{8,12},{12,8},{16,20},{20,16},{24,28},{28,24},{1,5},{5... | collective-permute-start | bytes 2359304 | tf_op jit(solution)/shard_map/ppermute | solution.py:298
  259.6 449.1 %collective-permute-start.56 = (bf16[384,512]{1,0:T(8,128)(2,1)}, bf16[384,512]{1,0:T(8,128)(2,1)}, u32[]{:S(2)}, u32[]{:S(2)}) collective-permute-start(bf16[384,512]{1,0:T(8,128)(2,1)} %get-tuple-element.100), channel_id=1, source_target_pairs={{0,4},{4,0},{8,12},{12,8},{16,20},{20,16},{24,28},{28,24},{1,5},{5... | collective-permute-start | bytes 1179656 | tf_op jit(solution)/shard_map/ppermute | solution.py:298
  266.0 283.7 %collective-permute-start.20 = (bf16[384,1024]{0,1:T(8,128)(2,1)}, bf16[384,1024]{0,1:T(8,128)(2,1)}, u32[]{:S(2)}, u32[]{:S(2)}) collective-permute-start(bf16[384,1024]{0,1:T(8,128)(2,1)} %bitcast.25), channel_id=1, source_target_pairs={{0,4},{4,0},{8,12},{12,8},{16,20},{20,16},{24,28},{28,24},{1,5},{5... | collective-permute-start | bytes 2359304 | tf_op jit(solution)/shard_map/ppermute | solution.py:298
  504.6 12.7 %collective-permute-start.35 = (f32[1024]{0:T(1024)}, f32[1024]{0:T(1024)S(1)}, u32[]{:S(2)}, u32[]{:S(2)}) collective-permute-start(f32[1024]{0:T(1024)} %get-tuple-element.48), channel_id=1, source_target_pairs={{0,4},{4,0},{8,12},{12,8},{16,20},{20,16},{24,28},{28,24},{1,5},{5... | collective-permute-start | bytes 12296 | tf_op jit(solution)/shard_map/ppermute | solution.py:298
  513.1 87.6 %all-to-all-start.5 = ((bf16[8,384,128]{2,1,0:T(8,128)(2,1)}), bf16[8,384,128]{2,1,0:T(8,128)(2,1)S(1)}, u32[]{:S(2)}, u32[]{:S(2)}) async-start(bf16[8,384,128]{2,1,0:T(8,128)(2,1)} %bitcast.533), calls=%async_computation.5 | async-start | bytes 1572864 | tf_op jit(solution)/shard_map/all_to_all | solution.py:428
  517.3 32.4 %collective-permute-start.21 = (bf16[384,512]{1,0:T(8,128)(2,1)S(1)}, bf16[384,512]{1,0:T(8,128)(2,1)}, u32[]{:S(2)}, u32[]{:S(2)}) collective-permute-start(bf16[384,512]{1,0:T(8,128)(2,1)S(1)} %get-tuple-element.102), channel_id=1, source_target_pairs={{0,4},{4,0},{8,12},{12,8},{16,20},{20,16},{24,28},{28,24},{1,5},{5... | collective-permute-start | bytes 1179656 | tf_op jit(solution)/shard_map/ppermute | solution.py:298
  518.0 10.1 %collective-permute-start.36 = (f32[1024]{0:T(1024)S(1)}, f32[1024]{0:T(1024)S(1)}, u32[]{:S(2)}, u32[]{:S(2)}) collective-permute-start(f32[1024]{0:T(1024)S(1)} %add.317), channel_id=1, source_target_pairs={{0,8},{4,12},{8,0},{12,4},{16,24},{20,28},{24,16},{28,20},{1,9},{5... | collective-permute-start | bytes 12296 | tf_op jit(solution)/shard_map/ppermute | solution.py:298
  544.0 135.2 %collective-permute-start.40 = (bf16[384,1024]{1,0:T(8,128)(2,1)}, bf16[384,1024]{1,0:T(8,128)(2,1)}, u32[]{:S(2)}, u32[]{:S(2)}) collective-permute-start(bf16[384,1024]{1,0:T(8,128)(2,1)} %multiply_convert_fusion.2), channel_id=1, source_target_pairs={{0,4},{4,0},{8,12},{12,8},{16,20},{20,16},{24,28},{28,24},{1,5},{5... | collective-permute-start | bytes 2359304 | tf_op jit(solution)/shard_map/ppermute | solution.py:298
  549.7 125.4 %collective-permute-start.41 = (bf16[384,2624]{0,1:T(8,128)(2,1)}, bf16[384,2624]{0,1:T(8,128)(2,1)}, u32[]{:S(2)}, u32[]{:S(2)}) collective-permute-start(bf16[384,2624]{0,1:T(8,128)(2,1)} %copy.501), channel_id=1, source_target_pairs={{0,4},{4,0},{8,12},{12,8},{16,20},{20,16},{24,28},{28,24},{1,5},{5... | collective-permute-start | bytes 6045704 | tf_op jit(solution)/shard_map/ppermute | solution.py:298
  552.3 7.4 collective-permute-start.28
  559.7 6.5 collective-permute-start.22
  601.6 64.3 %all-to-all-start.3 = ((bf16[8,48,1024]{2,1,0:T(8,128)(2,1)}), bf16[8,48,1024]{2,1,0:T(8,128)(2,1)S(1)}, u32[]{:S(2)}, u32[]{:S(2)}) async-start(bf16[8,48,1024]{2,1,0:T(8,128)(2,1)} %bitcast.27), calls=%async_computation.3 | async-start | bytes 1572864 | tf_op jit(solution)/shard_map/all_to_all | solution.py:428
  618.0 54.3 %collective-permute-start.34 = (bf16[256,512]{1,0:T(8,128)(2,1)S(1)}, bf16[256,512]{1,0:T(8,128)(2,1)S(1)}, u32[]{:S(2)}, u32[]{:S(2)}) collective-permute-start(bf16[256,512]{1,0:T(8,128)(2,1)S(1)} %bitcast.573), channel_id=1, source_target_pairs={{0,4},{4,0},{8,12},{12,8},{16,20},{20,16},{24,28},{28,24},{1,5},{5... | collective-permute-start | bytes 786440 | tf_op jit(solution)/shard_map/ppermute | solution.py:298
  665.9 86.3 %all-to-all-start.6 = ((bf16[8,384,384]{1,2,0:T(8,128)(2,1)}), bf16[8,384,384]{1,2,0:T(8,128)(2,1)}, u32[]{:S(2)}, u32[]{:S(2)}) async-start(bf16[8,384,384]{1,2,0:T(8,128)(2,1)} %copy.469), calls=%async_computation.6 | async-start | bytes 4718592 | tf_op jit(solution)/shard_map/all_to_all | solution.py:428
  673.0 31.6 %collective-permute-start.55 = (bf16[384,2624]{0,1:T(8,128)(2,1)}, bf16[384,2624]{0,1:T(8,128)(2,1)}, u32[]{:S(2)}, u32[]{:S(2)}) collective-permute-start(bf16[384,2624]{0,1:T(8,128)(2,1)} %copy.514), channel_id=1, source_target_pairs={{0,4},{4,0},{8,12},{12,8},{16,20},{20,16},{24,28},{28,24},{1,5},{5... | collective-permute-start | bytes 6045704 | tf_op jit(solution)/shard_map/ppermute | solution.py:298
  702.8 134.0 %collective-permute-start.48 = (bf16[2,2,2,32,2624]{4,3,0,1,2:T(8,128)(2,1)}, bf16[2,2,2,32,2624]{4,3,0,1,2:T(8,128)(2,1)}, u32[]{:S(2)}, u32[]{:S(2)}) collective-permute-start(bf16[2,2,2,32,2624]{4,3,0,1,2:T(8,128)(2,1)} %select_bitcast_fusion), channel_id=1, source_target_pairs={{0,16},{4,20},{8,24},{12,28},{16,0},{20,4},{24,8},{28,12},{1,17},{... | collective-permute-start | bytes 4030472 | tf_op jit(solution)/shard_map/ppermute | solution.py:298
  722.9 26.5 %collective-permute-start.63 = (bf16[2,2,2,328,128]{4,3,0,1,2:T(8,128)(2,1)S(1)}, bf16[2,2,2,328,128]{4,3,0,1,2:T(8,128)(2,1)S(1)}, u32[]{:S(2)}, u32[]{:S(2)}) collective-permute-start(bf16[2,2,2,328,128]{4,3,0,1,2:T(8,128)(2,1)S(1)} %select_bitcast_fusion.5), channel_id=1, source_target_pairs={{0,16},{4,20},{8,24},{12,28},{16,0},{20,4},{24,8},{28,12},{1,17},{... | collective-permute-start | bytes 2015240 | tf_op jit(solution)/shard_map/ppermute | solution.py:298
  727.3 112.6 %collective-permute-start.42 = (bf16[2,2,2,32,2624]{4,3,0,1,2:T(8,128)(2,1)}, bf16[2,2,2,32,2624]{4,3,0,1,2:T(8,128)(2,1)}, u32[]{:S(2)}, u32[]{:S(2)}) collective-permute-start(bf16[2,2,2,32,2624]{4,3,0,1,2:T(8,128)(2,1)} %select_bitcast_fusion.1), channel_id=1, source_target_pairs={{0,8},{4,12},{8,0},{12,4},{16,24},{20,28},{24,16},{28,20},{1,9},{5... | collective-permute-start | bytes 4030472 | tf_op jit(solution)/shard_map/ppermute | solution.py:298
  729.4 43.7 %collective-permute-start.57 = (bf16[2,2,2,328,128]{4,3,2,1,0:T(8,128)(2,1)}, bf16[2,2,2,328,128]{4,3,2,1,0:T(8,128)(2,1)}, u32[]{:S(2)}, u32[]{:S(2)}) collective-permute-start(bf16[2,2,2,328,128]{4,3,2,1,0:T(8,128)(2,1)} %fusion.70), channel_id=1, source_target_pairs={{0,8},{4,12},{8,0},{12,4},{16,24},{20,28},{24,16},{28,20},{1,9},{5... | collective-permute-start | bytes 2015240 | tf_op jit(solution)/shard_map/ppermute | solution.py:298
  750.5 49.1 %collective-permute-start.64 = (bf16[2,2,328,128]{3,2,0,1:T(8,128)(2,1)S(1)}, bf16[2,2,328,128]{3,2,0,1:T(8,128)(2,1)}, u32[]{:S(2)}, u32[]{:S(2)}) collective-permute-start(bf16[2,2,328,128]{3,2,0,1:T(8,128)(2,1)S(1)} %select_bitcast_fusion.13), channel_id=1, source_target_pairs={{0,8},{4,12},{8,0},{12,4},{16,24},{20,28},{24,16},{28,20},{1,9},{5... | collective-permute-start | bytes 1007624 | tf_op jit(solution)/shard_map/ppermute | solution.py:298
  785.4 12.2 %collective-permute-start.4 = (f32[1024]{0:T(1024)S(1)}, f32[1024]{0:T(1024)S(1)}, u32[]{:S(2)}, u32[]{:S(2)}) collective-permute-start(f32[1024]{0:T(1024)S(1)} %add.293), channel_id=1, source_target_pairs={{0,2},{1,3},{2,0},{3,1},{4,6},{5,7},{6,4},{7,5},{8,10},{9,11},{10,... | collective-permute-start | bytes 12296 | tf_op jit(solution)/shard_map/ppermute | solution.py:298
  789.6 58.2 %all-to-all-start.7 = ((bf16[8,48,1024]{2,1,0:T(8,128)(2,1)}), bf16[8,48,1024]{2,1,0:T(8,128)(2,1)}, u32[]{:S(2)}, u32[]{:S(2)}) async-start(bf16[8,48,1024]{2,1,0:T(8,128)(2,1)} %bitcast.555), calls=%async_computation.7 | async-start | bytes 1572864 | tf_op jit(solution)/shard_map/all_to_all | solution.py:428
  797.6 17.9 %collective-permute-start.58 = (bf16[2,2,328,128]{3,2,1,0:T(8,128)(2,1)}, bf16[2,2,328,128]{3,2,1,0:T(8,128)(2,1)S(1)}, u32[]{:S(2)}, u32[]{:S(2)}) collective-permute-start(bf16[2,2,328,128]{3,2,1,0:T(8,128)(2,1)} %fusion.83), channel_id=1, source_target_pairs={{0,16},{4,20},{8,24},{12,28},{16,0},{20,4},{24,8},{28,12},{1,17},{... | collective-permute-start | bytes 1007624 | tf_op jit(solution)/shard_map/ppermute | solution.py:298
  799.6 68.5 %collective-permute-start.6 = (bf16[384,1536]{0,1:T(8,128)(2,1)}, bf16[384,1536]{0,1:T(8,128)(2,1)}, u32[]{:S(2)}, u32[]{:S(2)}) collective-permute-start(bf16[384,1536]{0,1:T(8,128)(2,1)} %get-tuple-element.84), channel_id=1, source_target_pairs={{0,4},{4,0},{8,12},{12,8},{16,20},{20,16},{24,28},{28,24},{1,5},{5... | collective-permute-start | bytes 3538952 | tf_op jit(solution)/shard_map/ppermute | solution.py:298
  815.5 4.9 collective-permute-start.65
  820.4 4.2 collective-permute-start.59
  824.6 5.1 collective-permute-start.66
  829.7 5.0 collective-permute-start.60
  834.7 10.8 %collective-permute-start.67 = (bf16[328,128]{1,0:T(8,128)(2,1)S(1)}, bf16[328,128]{1,0:T(8,128)(2,1)S(1)}, u32[]{:S(2)}, u32[]{:S(2)}) collective-permute-start(bf16[328,128]{1,0:T(8,128)(2,1)S(1)} %fusion.98), channel_id=1, source_target_pairs={{0,8},{4,12},{8,0},{12,4},{16,24},{20,28},{24,16},{28,20},{1,9},{5... | collective-permute-start | bytes 251912 | tf_op jit(solution)/shard_map/ppermute | solution.py:298
  836.9 6.5 collective-permute-start.61
  839.9 34.8 %collective-permute-start.49 = (bf16[2,2,32,2624]{3,2,0,1:T(8,128)(2,1)}, bf16[2,2,32,2624]{3,2,0,1:T(8,128)(2,1)}, u32[]{:S(2)}, u32[]{:S(2)}) collective-permute-start(bf16[2,2,32,2624]{3,2,0,1:T(8,128)(2,1)} %select_bitcast_fusion.3), channel_id=1, source_target_pairs={{0,8},{4,12},{8,0},{12,4},{16,24},{20,28},{24,16},{28,20},{1,9},{5... | collective-permute-start | bytes 2015240 | tf_op jit(solution)/shard_map/ppermute | solution.py:298
  843.4 32.9 %collective-permute-start.43 = (bf16[2,2,32,2624]{3,2,0,1:T(8,128)(2,1)}, bf16[2,2,32,2624]{3,2,0,1:T(8,128)(2,1)}, u32[]{:S(2)}, u32[]{:S(2)}) collective-permute-start(bf16[2,2,32,2624]{3,2,0,1:T(8,128)(2,1)} %select_bitcast_fusion.4), channel_id=1, source_target_pairs={{0,16},{4,20},{8,24},{12,28},{16,0},{20,4},{24,8},{28,12},{1,17},{... | collective-permute-start | bytes 2015240 | tf_op jit(solution)/shard_map/ppermute | solution.py:298
  845.5 12.4 %collective-permute-start.62 = (bf16[2,328,128]{2,1,0:T(8,128)(2,1)}, bf16[2,328,128]{2,1,0:T(8,128)(2,1)}, u32[]{:S(2)}, u32[]{:S(2)}) collective-permute-start(bf16[2,328,128]{2,1,0:T(8,128)(2,1)} %pad_maximum_fusion.15), channel_id=1, source_target_pairs={{0,8},{4,12},{8,0},{12,4},{16,24},{20,28},{24,16},{28,20},{1,9},{5... | collective-permute-start | bytes 503816 | tf_op jit(solution)/shard_map/ppermute | solution.py:298
  857.9 4.6 collective-permute-start.68
  862.7 16.5 %collective-permute-start.69 = (bf16[656,512]{1,0:T(8,128)(2,1)S(1)}, bf16[656,512]{1,0:T(8,128)(2,1)S(1)}, u32[]{:S(2)}, u32[]{:S(2)}) collective-permute-start(bf16[656,512]{1,0:T(8,128)(2,1)S(1)} %copy_bitcast_fusion.1), channel_id=1, source_target_pairs={{0,4},{4,0},{8,12},{12,8},{16,20},{20,16},{24,28},{28,24},{1,5},{5... | collective-permute-start | bytes 2015240 | tf_op jit(solution)/shard_map/ppermute | solution.py:298
  873.0 39.3 %collective-permute-start.13 = (bf16[2,2,2,32,1536]{4,3,2,1,0:T(8,128)(2,1)S(1)}, bf16[2,2,2,32,1536]{4,3,2,1,0:T(8,128)(2,1)S(1)}, u32[]{:S(2)}, u32[]{:S(2)}) collective-permute-start(bf16[2,2,2,32,1536]{4,3,2,1,0:T(8,128)(2,1)S(1)} %fusion.55), channel_id=1, source_target_pairs={{0,16},{4,20},{8,24},{12,28},{16,0},{20,4},{24,8},{28,12},{1,17},{... | collective-permute-start | bytes 2359304 | tf_op jit(solution)/shard_map/ppermute | solution.py:298
  873.8 39.5 %collective-permute-start.7 = (bf16[2,2,2,32,1536]{4,3,0,1,2:T(8,128)(2,1)S(1)}, bf16[2,2,2,32,1536]{4,3,0,1,2:T(8,128)(2,1)S(1)}, u32[]{:S(2)}, u32[]{:S(2)}) collective-permute-start(bf16[2,2,2,32,1536]{4,3,0,1,2:T(8,128)(2,1)S(1)} %select_bitcast_fusion.2), channel_id=1, source_target_pairs={{0,8},{4,12},{8,0},{12,4},{16,24},{20,28},{24,16},{28,20},{1,9},{5... | collective-permute-start | bytes 2359304 | tf_op jit(solution)/shard_map/ppermute | solution.py:298
  876.2 9.1 collective-permute-start.50
  877.7 17.9 %collective-permute-start.44 = (bf16[2,32,2624]{2,1,0:T(8,128)(2,1)S(1)}, bf16[2,32,2624]{2,1,0:T(8,128)(2,1)S(1)}, u32[]{:S(2)}, u32[]{:S(2)}) collective-permute-start(bf16[2,32,2624]{2,1,0:T(8,128)(2,1)S(1)} %select_bitcast_fusion.12), channel_id=1, source_target_pairs={{0,1},{1,0},{2,3},{3,2},{4,5},{5,4},{6,7},{7,6},{8,9},{9,8},{10,11... | collective-permute-start | bytes 1007624 | tf_op jit(solution)/shard_map/ppermute | solution.py:298
  885.4 10.4 %collective-permute-start.51 = (bf16[32,2624]{1,0:T(8,128)(2,1)S(1)}, bf16[32,2624]{1,0:T(8,128)(2,1)S(1)}, u32[]{:S(2)}, u32[]{:S(2)}) collective-permute-start(bf16[32,2624]{1,0:T(8,128)(2,1)S(1)} %select_bitcast_fusion.22), channel_id=1, source_target_pairs={{0,2},{1,3},{2,0},{3,1},{4,6},{5,7},{6,4},{7,5},{8,10},{9,11},{10,... | collective-permute-start | bytes 503816 | tf_op jit(solution)/shard_map/ppermute | solution.py:298
  895.8 9.9 %collective-permute-start.45 = (bf16[32,2624]{1,0:T(8,128)(2,1)S(1)}, bf16[32,2624]{1,0:T(8,128)(2,1)S(1)}, u32[]{:S(2)}, u32[]{:S(2)}) collective-permute-start(bf16[32,2624]{1,0:T(8,128)(2,1)S(1)} %select_bitcast_fusion.25), channel_id=1, source_target_pairs={{0,2},{1,3},{2,0},{3,1},{4,6},{5,7},{6,4},{7,5},{8,10},{9,11},{10,... | collective-permute-start | bytes 503816 | tf_op jit(solution)/shard_map/ppermute | solution.py:298
  896.0 10.1 %collective-permute-start.52 = (bf16[32,2624]{1,0:T(8,128)(2,1)S(1)}, bf16[32,2624]{1,0:T(8,128)(2,1)S(1)}, u32[]{:S(2)}, u32[]{:S(2)}) collective-permute-start(bf16[32,2624]{1,0:T(8,128)(2,1)S(1)} %fusion.81), channel_id=1, source_target_pairs={{0,8},{4,12},{8,0},{12,4},{16,24},{20,28},{24,16},{28,20},{1,9},{5... | collective-permute-start | bytes 503816 | tf_op jit(solution)/shard_map/ppermute | solution.py:298
  905.8 5.5 collective-permute-start.46
  906.1 12.5 %collective-permute-start.53 = (bf16[2,32,2624]{2,1,0:T(8,128)(2,1)S(1)}, bf16[2,32,2624]{2,1,0:T(8,128)(2,1)S(1)}, u32[]{:S(2)}, u32[]{:S(2)}) collective-permute-start(bf16[2,32,2624]{2,1,0:T(8,128)(2,1)S(1)} %pad_maximum_fusion.9), channel_id=1, source_target_pairs={{0,16},{4,20},{8,24},{12,28},{16,0},{20,4},{24,8},{28,12},{1,17},{... | collective-permute-start | bytes 1007624 | tf_op jit(solution)/shard_map/ppermute | solution.py:298
  911.4 7.5 collective-permute-start.47
  912.7 16.3 %collective-permute-start.14 = (bf16[2,2,32,1536]{3,2,1,0:T(8,128)(2,1)S(1)}, bf16[2,2,32,1536]{3,2,1,0:T(8,128)(2,1)S(1)}, u32[]{:S(2)}, u32[]{:S(2)}) collective-permute-start(bf16[2,2,32,1536]{3,2,1,0:T(8,128)(2,1)S(1)} %fusion.77), channel_id=1, source_target_pairs={{0,8},{4,12},{8,0},{12,4},{16,24},{20,28},{24,16},{28,20},{1,9},{5... | collective-permute-start | bytes 1179656 | tf_op jit(solution)/shard_map/ppermute | solution.py:298
  914.4 14.3 %collective-permute-start.8 = (bf16[2,2,32,1536]{3,2,0,1:T(8,128)(2,1)}, bf16[2,2,32,1536]{3,2,0,1:T(8,128)(2,1)S(1)}, u32[]{:S(2)}, u32[]{:S(2)}) collective-permute-start(bf16[2,2,32,1536]{3,2,0,1:T(8,128)(2,1)} %select_bitcast_fusion.6), channel_id=1, source_target_pairs={{0,16},{4,20},{8,24},{12,28},{16,0},{20,4},{24,8},{28,12},{1,17},{... | collective-permute-start | bytes 1179656 | tf_op jit(solution)/shard_map/ppermute | solution.py:298
  922.9 37.4 %collective-permute-start.54 = (bf16[256,2624]{0,1:T(8,128)(2,1)}, bf16[256,2624]{0,1:T(8,128)(2,1)S(1)}, u32[]{:S(2)}, u32[]{:S(2)}) collective-permute-start(bf16[256,2624]{0,1:T(8,128)(2,1)} %copy.511), channel_id=1, source_target_pairs={{0,4},{4,0},{8,12},{12,8},{16,20},{20,16},{24,28},{28,24},{1,5},{5... | collective-permute-start | bytes 4030472 | tf_op jit(solution)/shard_map/ppermute | solution.py:298
  928.9 6.5 collective-permute-start.9
  929.2 11.5 %collective-permute-start.15 = (bf16[2,32,1536]{2,1,0:T(8,128)(2,1)S(1)}, bf16[2,32,1536]{2,1,0:T(8,128)(2,1)S(1)}, u32[]{:S(2)}, u32[]{:S(2)}) collective-permute-start(bf16[2,32,1536]{2,1,0:T(8,128)(2,1)S(1)} %fusion.92), channel_id=1, source_target_pairs={{0,1},{1,0},{2,3},{3,2},{4,5},{5,4},{6,7},{7,6},{8,9},{9,8},{10,11... | collective-permute-start | bytes 589832 | tf_op jit(solution)/shard_map/ppermute | solution.py:298
  935.5 5.3 collective-permute-start.10
  940.8 7.2 collective-permute-start.16
  940.9 8.0 collective-permute-start.11
  948.9 7.2 collective-permute-start.12
  952.0 4.9 collective-permute-start.18
  957.1 12.2 %collective-permute-start.19 = (bf16[256,1536]{1,0:T(8,128)(2,1)S(1)}, bf16[256,1536]{1,0:T(8,128)(2,1)S(1)}, u32[]{:S(2)}, u32[]{:S(2)}) collective-permute-start(bf16[256,1536]{1,0:T(8,128)(2,1)S(1)} %bitcast.561), channel_id=1, source_target_pairs={{0,4},{4,0},{8,12},{12,8},{16,20},{20,16},{24,28},{28,24},{1,5},{5... | collective-permute-start | bytes 2359304 | tf_op jit(solution)/shard_map/ppermute | solution.py:298
  (75 other events, 758.0 us)
Sparse Core Ops, SparseCore 0:
  9.6 117.6 all-gather.6
  128.8 43.4 all-gather.8
  173.9 187.3 all-gather.10
  362.8 98.2 all-gather.12

commit v2 on v1

--- a/solution.py
+++ b/solution.py
@@ -278,6 +278,182 @@
     )
 
 
+def toggled(index, bit):
+    return index + bit - 2 * bit * ((index // bit) % 2)
+
+
+def gather_kernel(shapes, *refs):
+    count = len(shapes)
+    shard_refs, full_refs = (refs[:count], refs[count : 2 * count])
+    send_sem, recv_sem, local_sem = refs[2 * count :]
+    shards = lax.axis_size("fsdp")
+    slices = lax.axis_size("ctx") // 2
+    own_ctx, own_shard = (lax.axis_index("ctx"), lax.axis_index("fsdp"))
+    core, chip = (own_ctx % 2, own_ctx // 2)
+    barrier = pltpu.get_barrier_semaphore()
+    partners = [{"fsdp": toggled(own_shard, bit)} for bit in (1, 2)]
+    partners += [{"ctx": toggled(own_ctx, bit)} for bit in (1, 2, 4)]
+    for partner in partners:
+        pl.semaphore_signal(
+            barrier, inc=1, device_id=partner, device_id_type=pl.DeviceIdType.MESH
+        )
+    pl.semaphore_wait(barrier, len(partners))
+    to_one, to_two, to_core, to_x, to_y = partners
+
+    def shard_at(step):
+        if step == 0:
+            return own_shard
+        if step == 3:
+            return toggled(toggled(own_shard, 1), 2)
+        return toggled(own_shard, step)
+
+    def region(ref, weight, step, chip_at, half):
+        if shapes[weight] == "small":
+            return ref if len(ref.shape) == 2 else ref.at[shard_at(step)]
+        if shapes[weight] == "rows":
+            rows = ref.shape[-2]
+            span = pl.ds(0, rows) if half is None else pl.ds(half * (rows // 2), rows // 2)
+            if len(ref.shape) == 4:
+                return ref.at[core, chip_at, span, :]
+            return ref.at[shard_at(step), core, chip_at, span, :]
+        rows = ref.shape[-2]
+        first = (rows // 2) // 16 * 16
+        spans_of = {None: pl.ds(0, rows), 0: pl.ds(0, first), 1: pl.ds(first, rows - first)}
+        width = ref.shape[-1] // (2 * slices)
+        columns = pl.ds(pl.multiple_of((core * slices + chip_at) * width, width), width)
+        if len(ref.shape) == 2:
+            return ref.at[spans_of[half], columns]
+        return ref.at[shard_at(step), spans_of[half], columns]
+
+    def core_region(ref, weight, step):
+        if shapes[weight] == "rows":
+            return ref.at[shard_at(step), core]
+        width = ref.shape[-1] // 2
+        return ref.at[shard_at(step), :, pl.ds(pl.multiple_of(core * width, width), width)]
+
+    pending = []
+
+    def send(source, target, slot, partner):
+        copy = pltpu.make_async_remote_copy(
+            src_ref=source,
+            dst_ref=target,
+            send_sem=send_sem.at[slot],
+            recv_sem=recv_sem.at[slot],
+            device_id=partner,
+            device_id_type=pl.DeviceIdType.MESH,
+        )
+        copy.start()
+        pending.append(copy)
+        return copy
+
+    copies = {}
+    local = []
+
+    def slot_of(weight, step, kind):
+        return (weight * 3 + step - 1) * 8 + kind
+
+    def shard_sends(weight):
+        source = region(shard_refs[weight], weight, 0, chip, None)
+        target = region(full_refs[weight], weight, 0, chip, None)
+        copies[weight, 2, 0] = send(source, target, slot_of(weight, 2, 0), to_two)
+        copies[weight, 1, 0] = send(source, target, slot_of(weight, 1, 0), to_one)
+        target = full_refs[weight].at[own_shard]
+        copy = pltpu.make_async_copy(shard_refs[weight], target, local_sem.at[weight])
+        copy.start()
+        local.append(copy)
+
+    def shard_forward(weight):
+        copies[weight, 2, 0].wait_recv()
+        piece = region(full_refs[weight], weight, 2, chip, None)
+        copies[weight, 3, 0] = send(piece, piece, slot_of(weight, 3, 0), to_one)
+
+    def plane_sends(weight, step):
+        lead = region(full_refs[weight], weight, step, chip, 0)
+        rest = region(full_refs[weight], weight, step, chip, 1)
+        for kind, piece, partner in ((1, lead, to_x), (2, rest, to_y), (3, lead, to_y), (4, rest, to_x)):
+            copies[weight, step, kind] = send(piece, piece, slot_of(weight, step, kind), partner)
+
+    def plane_forward(weight, step):
+        copies[weight, step, 1].wait_recv()
+        lead = region(full_refs[weight], weight, step, toggled(chip, 1), 0)
+        copies[weight, step, 5] = send(lead, lead, slot_of(weight, step, 5), to_y)
+        copies[weight, step, 2].wait_recv()
+        rest = region(full_refs[weight], weight, step, toggled(chip, 2), 1)
+        copies[weight, step, 6] = send(rest, rest, slot_of(weight, step, 6), to_x)
+
+    def core_send(weight, step):
+        for kind in (3, 4, 5, 6):
+            copies[weight, step, kind].wait_recv()
+        piece = core_region(full_refs[weight], weight, step)
+        copies[weight, step, 7] = send(piece, piece, slot_of(weight, step, 7), to_core)
+
+    shard_sends(0)
+    for weight in range(count):
+        if weight + 1 < count:
+            shard_sends(weight + 1)
+        shard_forward(weight)
+        copies[weight, 1, 0].wait_recv()
+        if shapes[weight] == "small":
+            copies[weight, 3, 0].wait_recv()
+            continue
+        plane_sends(weight, 1)
+        plane_sends(weight, 2)
+        copies[weight, 3, 0].wait_recv()
+        plane_sends(weight, 3)
+        for step in (1, 2, 3):
+            plane_forward(weight, step)
+        if weight > 0 and shapes[weight - 1] != "small":
+            for step in (1, 2, 3):
+                core_send(weight - 1, step)
+    for step in (1, 2, 3):
+        core_send(count - 1, step)
+    for weight in range(count):
+        if shapes[weight] != "small":
+            for step in (1, 2, 3):
+                copies[weight, step, 7].wait_recv()
+    for copy in pending:
+        copy.wait_send()
+    for copy in local:
+        copy.wait()
+
+
+def gather_weights(weights):
+    shards, ctx_count = (lax.axis_size("fsdp"), lax.axis_size("ctx"))
+    slices = ctx_count // 2
+    shapes, views, outs = ([], [], [])
+    for weight in weights:
+        rows, columns = weight.shape
+        if rows % (32 * ctx_count) == 0:
+            shapes.append("rows")
+            views.append(weight.reshape(2, slices, rows // ctx_count, columns))
+            outs.append((shards, 2, slices, rows // ctx_count, columns))
+        elif rows == 16:
+            shapes.append("small")
+            views.append(weight)
+            outs.append((shards, rows, columns))
+        elif columns % (128 * ctx_count) == 0 and rows % 16 == 0:
+            shapes.append("columns")
+            views.append(weight)
+            outs.append((shards, rows, columns))
+    if shards != 4 or ctx_count != 8 or len(views) < len(weights):
+        return [lax.all_gather(weight, "fsdp", axis=0, tiled=True) for weight in weights]
+    slots = len(views) * 24
+    held = pl.pallas_call(
+        functools.partial(gather_kernel, shapes),
+        out_shape=tuple(jax.ShapeDtypeStruct(out, jnp.bfloat16) for out in outs),
+        in_specs=[pl.BlockSpec(memory_space=pltpu.VMEM)] * len(views),
+        out_specs=tuple(pl.BlockSpec(memory_space=pl.ANY) for out in outs),
+        scratch_shapes=[
+            pltpu.SemaphoreType.DMA((slots,)),
+            pltpu.SemaphoreType.DMA((slots,)),
+            pltpu.SemaphoreType.DMA((len(views),)),
+        ],
+        compiler_params=pltpu.CompilerParams(collective_id=0, has_side_effects=True),
+        name="gather_weights",
+    )(*views)
+    return [whole.reshape(-1, whole.shape[-1]) for whole in held]
+
+
 def layer_norm(rows_in, gain_vec):
     row_mean = jnp.mean(rows_in, axis=-1, keepdims=True)
     centred = rows_in - row_mean
@@ -448,17 +624,13 @@
     grad_final = jnp.where(
         is_valid[:, None], grad_arrived.reshape(row_count, model_width).astype(jnp.float32), 0.0
     )
-    gain_attn_low, qkv_full, attn_full = (
-        lax.all_gather(gain_one, "fsdp", axis=0, tiled=True),
-        lax.all_gather(qkv_weight, "fsdp", axis=0, tiled=True),
-        lax.all_gather(attn_out, "fsdp", axis=0, tiled=True),
-    )
-    gain_mlp_low, in_full, out_full = (
-        lax.all_gather(gain_two, "fsdp", axis=0, tiled=True),
-        lax.all_gather(geglu_in, "fsdp", axis=0, tiled=True),
-        lax.all_gather(geglu_out, "fsdp", axis=0, tiled=True),
-    )
-    gain_attn = gain_attn_low.astype(jnp.float32)
+    gains = jnp.pad(jnp.stack([gain_one, gain_two]), ((0, 14), (0, 0)))
+    gains_full, qkv_full, attn_full, in_full, out_full = gather_weights(
+        [gains, qkv_weight, attn_out, geglu_in, geglu_out]
+    )
+    gains_full = gains_full.reshape(-1, 16, gains.shape[1])
+    gain_attn = gains_full[:, 0].reshape(-1).astype(jnp.float32)
+    gain_mlp = gains_full[:, 1].reshape(-1).astype(jnp.float32)
     act_attn = layer_norm(residual, gain_attn).astype(jnp.bfloat16)
     projected = jnp.dot(act_attn, qkv_full, preferred_element_type=jnp.float32)
     cosine, sine = rotary_tables(offset, 1)
@@ -481,7 +653,6 @@
     )
     branch_attn = jnp.dot(attn_low, attn_full, preferred_element_type=jnp.float32)
     middle = residual + branch_attn
-    gain_mlp = gain_mlp_low.astype(jnp.float32)
     act_mlp = layer_norm(middle, gain_mlp).astype(jnp.bfloat16)
     up_both = jnp.dot(act_mlp, in_full, preferred_element_type=jnp.float32)
     ff_width = up_both.shape[1] // 2

time: 984 us -> 711 us (0.72)
  waiting for transfers between devices: 473 us -> 128 us
  Pallas kernels: 73.6 us -> 177 us
  matrix products: 92.1 us -> 72.4 us
  blocking collectives: 16.1 us -> 0 us
  between operations: 16.2 us -> 3.31 us
  other arithmetic: 86.5 us -> 96.6 us
  starting transfers between devices: 124 us -> 134 us
    all_gather x4 -> x0, waiting for transfers between devices: 267 us -> none  [the longest x1 93.1 us: per_device(): lax.all_gather(qkv_weight, 'fsdp', axis=0, tiled=True)]
    pallas_call x0 -> x1, Pallas kernels: none -> 105 us  [gather_weights(): pl.pallas_call(functools.partial(gather_kernel, shapes), out_shape=tuple(...]
    ppermute x73, waiting for transfers between devices: 182 us -> 113 us  [swap(): return lax.ppermute(value, axis, pairs)]
    ppermute x73, starting transfers between devices: 67.1 us -> 85.9 us  [swap(): return lax.ppermute(value, axis, pairs)]
    all_gather x2 -> x0, blocking collectives: 16.1 us -> none  [the longest x1 9.46 us: per_device(): lax.all_gather(gain_one, 'fsdp', axis=0, tiled=True)]
  transfers between devices with their start and end apart: 85 -> 81, of which waited for: 46 -> 34; matrix products, arithmetic and copies ran while one was open for 27% -> 31% of each run, Pallas kernels for 8% -> 25%
where the time goes in v2:
time: 711 us; the launch traced here: 701 us
  Pallas kernels  177 us (25%)
  starting transfers between devices  134 us (19%)
  waiting for transfers between devices  128 us (18%)
  other arithmetic  96.6 us (14%)
  local copies, waits for them, and re-layouts  89.2 us (13%)
  matrix products  72.4 us (10%)
    ppermute x73, waiting for transfers between devices, swap(): return lax.ppermute(value, axis, pairs)  113 us
    pallas_call x1, Pallas kernels, gather_weights(): pl.pallas_call(functools.partial(gather_kernel, shapes), out_shape=tuple(...  105 us
    ppermute x73, starting transfers between devices, swap(): return lax.ppermute(value, axis, pairs)  85.9 us
    all_to_all x8, starting transfers between devices, exchange(): lax.all_to_all(blocks, 'ctx', split_axis=0, concat_axis=0, tiled=True)  48.3 us
    pallas_call x1, Pallas kernels, attention_backward(): pl.pallas_call(functools.partial(backward_kernel, head_count, block_q, bl...  42.5 us
    pallas_call x1, Pallas kernels, attention_forward(): pl.pallas_call(functools.partial(forward_kernel, head_count, block_q, blo...  29.5 us
    dot_general x4, matrix products, core_product(): lax.dot_general(left_all, right_all, (((0,), (0,)), ((), ())), preferred_...  21.7 us
    all_to_all x8, waiting for transfers between devices, exchange(): lax.all_to_all(blocks, 'ctx', split_axis=0, concat_axis=0, tiled=True)  15 us
  transfers between devices with their start and end apart: 81, of which 34 were waited for; matrix products, arithmetic and copies ran while one was open for 31% of the time, Pallas kernels for 25%

profile of v2, /device:TPU:1, one launch (start us, length us, event | category | flops | bytes accessed | tf_op | source)
XLA Modules:
  0.0 700.5 jit_solution(14785772524188577834)
XLA Ops:
  4.4 5.3 all-to-all-start
  14.2 105.2 %gather_weights.1 = (bf16[4,16,256]{2,1,0:T(8,128)(2,1)}, bf16[4,2,4,32,3072]{4,3,2,1,0:T(8,128)(2,1)}, bf16[4,2,4,32,1024]{4,3,2,1,0:T(8,128)(2,1)}, bf16[4,2,4...) custom-call(bf16[16,256]{1,0:T(8,128)(2,1)} %fusion.114.refs_0_, bf16[2,4,32,3072]{3,2,1,0:T(8,128)(2,1)} %bitcast.589, ...), custom_call_target="tpu_custom_call" | custom-call | tf_op jit(solution)/shard_map/gather_weights/pallas_call | solution.py:441
  121.6 4.7 fusion.143
  129.7 3.0 copy.455
  132.7 3.0 copy.458
  139.7 3.0 copy.456
  142.8 3.0 copy.459
  145.8 3.7 fusion.58
  152.2 4.5 all-to-all-start.1
  160.5 7.1 %multiply_sine_fusion = (f32[3072,32]{1,0:T(8,128)S(1)}, f32[3072,32]{1,0:T(8,128)}, f32[3072,32]{1,0:T(8,128)}) fusion(f32[3072]{0:T(1024)S(1)} %subtract_convert_fusion.2, f32[32]{0:T(128)S(1)} %multiply_power_fusion), kind=kLoop, calls=%fused_computation.49 | loop fusion | flops 196608 | bytes 1192064 | tf_op jit(solution)/shard_map/sin | solution.py:274
  167.6 15.0 %all-to-all-done.1 = bf16[8,384,384]{2,1,0:T(8,128)(2,1)} async-done(((bf16[8,384,384]{2,1,0:T(8,128)(2,1)}), bf16[8,384,384]{2,1,0:T(8,128)(2,1)}, u32[]{:S(2)}, u32[]{:S(2)}) %all-to-all-start.1) | async-done | bytes 2359328 | tf_op jit(solution)/shard_map/all_to_all | solution.py:604
  182.6 7.2 %all-to-all-start.4 = ((bf16[8,48,1024]{2,1,0:T(8,128)(2,1)}), bf16[8,48,1024]{2,1,0:T(8,128)(2,1)S(1)}, u32[]{:S(2)}, u32[]{:S(2)}) async-start(bf16[8,48,1024]{2,1,0:T(8,128)(2,1)} %get-tuple-element.172), calls=%async_computation.4 | async-start | bytes 1572864 | tf_op jit(solution)/shard_map/all_to_all | solution.py:604
  191.1 29.5 %attention_forward.1 = (f32[3072,128]{1,0:T(8,128)}, f32[12,1,512]{2,1,0:T(1,128)}) custom-call(s32[12]{0:T(128)} %get-tuple-element.166.low_ref, s32[12]{0:T(128)} %get-tuple-element.167.high_ref, s32[1,3072]{1,0:T(1,128)} %get-tuple-element.178.begin_ref, s32[1,3072]{1,0:T(1,128)} %get-tuple-element.177.end_ref, bf16[3072,384]{1,0:T(8,128)(2,1)} %bitcast.27.qkv_ref), custom_call_target="tpu_custom_call" | custom-call | flops 2415919104 | bytes 4718592 | tf_op jit(solution)/shard_map/attention_forward/pallas_call | solution.py:97
  225.2 4.2 all-to-all-start.2
  230.9 8.6 %pad_maximum_fusion = (f32[3072,128]{1,0:T(8,128)}, f32[3072,128]{1,0:T(8,128)}) fusion(f32[3072,32]{1,0:T(8,128)} %get-tuple-element.158, f32[3072,32]{1,0:T(8,128)} %get-tuple-element.157, f32[3072,32]{1,0:T(8,128)S(1)} %get-tuple-element.156), kind=kLoop, calls=%fused_computation.56 | loop fusion | flops 2359296 | bytes 4325376 | tf_op jit(solution)/shard_map/concatenate | solution.py:276
  242.1 2.9 fusion.129
  246.5 8.1 %fusion.144 = f32[384,5248]{1,0:T(8,128)S(1)} fusion(bf16[384,1024]{1,0:T(8,128)(2,1)} %multiply_convert_fusion.2, bf16[1024,5248]{1,0:T(8,128)(2,1)} %bitcast.615), kind=kOutput, calls=%fused_computation.398 | convolution fusion | flops 4127195136 | bytes 19595264 | tf_op jit(solution)/shard_map/dot_general | solution.py:657
  254.7 14.1 %broadcast_select_fusion.1 = (bf16[384,2624]{1,0:T(8,128)(2,1)}, bf16[384,2624]{1,0:T(8,128)(2,1)S(1)}, bf16[384,2624]{1,0:T(8,128)(2,1)}, f32[384,2624]{1,0:T(8,128)S(1)}) fusion(pred[]{:T(512)S(6)} %eq.142, f32[384,5248]{1,0:T(8,128)S(1)} %fusion.144, bf16[384,1024]{1,0:T(8,128)(2,1)S(1)} %bitcast.595, bf16[2624,1024]{1,0:T(8,128)(2,1)S(1)} %bitcast.621), kind=kOutput, calls=%fused_computation.52 | convolution fusion | flops 2141184000 | bytes 24297472 | tf_op jit(solution)/shard_map/dot_general | solution.py:677
  268.8 8.4 %fusion.12 = f32[384,1024]{1,0:T(8,128)S(1)} fusion(bf16[1024,5248]{1,0:T(8,128)(2,1)} %bitcast.616, bf16[384,2624]{1,0:T(8,128)(2,1)} %get-tuple-element.66, bf16[384,2624]{1,0:T(8,128)(2,1)S(1)} %get-tuple-element.65), kind=kOutput, calls=%fused_computation.30 | convolution fusion | flops 4135256064 | bytes 16351232 | tf_op jit(solution)/shard_map/dot_general | solution.py:692
  278.7 5.6 multiply_convert_fusion.1
  284.4 4.5 multiply_reduce_fusion
  296.4 4.1 copy.514
  302.7 4.6 all-to-all-start.5
  307.4 4.0 copy.501
  325.5 4.4 collective-permute-start.38
  337.7 4.5 collective-permute-start.55
  347.1 6.2 collective-permute-done.28
  373.4 10.7 %all-to-all-start.3 = ((bf16[8,48,1024]{2,1,0:T(8,128)(2,1)}), bf16[8,48,1024]{2,1,0:T(8,128)(2,1)}, u32[]{:S(2)}, u32[]{:S(2)}) async-start(bf16[8,48,1024]{2,1,0:T(8,128)(2,1)} %bitcast.593), calls=%async_computation.3 | async-start | bytes 1572864 | tf_op jit(solution)/shard_map/all_to_all | solution.py:604
  384.3 42.5 %attention_backward.1 = bf16[3072,384]{1,0:T(8,128)(2,1)} custom-call(s32[12]{0:T(128)} %get-tuple-element.70.low_ref, s32[12]{0:T(128)} %get-tuple-element.71.high_ref, s32[1,3072]{1,0:T(1,128)} %get-tuple-element.178.begin_ref, s32[1,3072]{1,0:T(1,128)} %get-tuple-element.177.end_ref, bf16[3072,384]{1,0:T(8,128)(2,1)} %bitcast.27.qkv_ref, ...), custom_call_target="tpu_custom_call" | custom-call | flops 6039797760 | bytes 11796480 | tf_op jit(solution)/shard_map/attention_backward/pallas_call | solution.py:223
  426.8 4.3 copy.469
  431.1 4.8 all-to-all-start.6
  435.9 2.7 gather_fusion.1
  440.7 4.1 copy.502
  444.8 9.5 %convolution_convert_fusion = bf16[1024,2624]{0,1:T(8,128)(2,1)} fusion(bf16[384,2624]{1,0:T(8,128)(2,1)} %copy.502, bf16[384,2624]{1,0:T(8,128)(2,1)} %get-tuple-element.64, bf16[384,1024]{1,0:T(8,128)(2,1)} %collective-permute-done.40, bf16[384,1024]{1,0:T(8,128)(2,1)} %multiply_convert_fusion.2), kind=kOutput, calls=%fused_computation.5 | convolution fusion | flops 4141088768 | bytes 10977280 | tf_op jit(solution)/shard_map/dot_general | solution.py:521
  454.3 8.2 %copy.503 = bf16[1024,2624]{1,0:T(8,128)(2,1)} copy(bf16[1024,2624]{0,1:T(8,128)(2,1)} %convolution_convert_fusion) | data formatting | bytes 10747904 | tf_op jit(solution)/shard_map/convert_element_type | solution.py:523
  462.5 3.0 fusion.130
  472.9 6.0 fusion.46
  483.2 4.1 copy.515
  487.6 25.9 %collective-permute-done.1 = f32[1024]{0:T(1024)S(1)} collective-permute-done((f32[1024]{0:T(1024)S(1)}, f32[1024]{0:T(1024)S(1)}, u32[]{:S(2)}, u32[]{:S(2)}) %collective-permute-start.1) | collective-permute-done | bytes 4128 | tf_op jit(solution)/shard_map/ppermute | solution.py:474
  513.9 3.1 fusion.42
  523.3 7.0 all-to-all-start.7
  531.4 5.4 convolution_convert_fusion.1
  536.8 4.8 reshape.587
  553.1 2.7 gather_fusion.3
  555.8 2.8 broadcast_select_fusion.6
  565.6 4.4 convolution_convert_fusion.2
  572.0 4.6 collective-permute-done.49
  580.1 3.5 collective-permute-done.64
  585.5 11.8 %collective-permute-done.65 = bf16[2,328,128]{2,1,0:T(8,128)(2,1)S(1)} collective-permute-done((bf16[2,328,128]{2,1,0:T(8,128)(2,1)S(1)}, bf16[2,328,128]{2,1,0:T(8,128)(2,1)S(1)}, u32[]{:S(2)}, u32[]{:S(2)}) %collective-permute-start.65) | collective-permute-done | bytes 167968 | tf_op jit(solution)/shard_map/ppermute | solution.py:474
  598.0 3.8 collective-permute-done.59
  605.2 2.7 collective-permute-done.66
  607.8 7.0 %collective-permute-done.60 = bf16[328,128]{1,0:T(8,128)(2,1)S(1)} collective-permute-done((bf16[328,128]{1,0:T(8,128)(2,1)S(1)}, bf16[328,128]{1,0:T(8,128)(2,1)S(1)}, u32[]{:S(2)}, u32[]{:S(2)}) %collective-permute-start.60) | collective-permute-done | bytes 84000 | tf_op jit(solution)/shard_map/ppermute | solution.py:474
  614.9 2.9 collective-permute-start.67
  621.0 2.6 collective-permute-done.61
  631.0 7.0 %collective-permute-start.69 = (bf16[656,512]{1,0:T(8,128)(2,1)}, bf16[656,512]{1,0:T(8,128)(2,1)}, u32[]{:S(2)}, u32[]{:S(2)}) collective-permute-start(bf16[656,512]{1,0:T(8,128)(2,1)} %copy_bitcast_fusion.1), channel_id=1, source_target_pairs={{0,4},{4,0},{8,12},{12,8},{16,20},{20,16},{24,28},{28,24},{1,5},{5... | collective-permute-start | bytes 2015240 | tf_op jit(solution)/shard_map/ppermute | solution.py:474
  643.5 4.3 collective-permute-done.53
  649.3 2.7 copy.511
  652.0 4.2 collective-permute-start.54
  662.0 4.7 collective-permute-done.9
  670.2 4.4 collective-permute-done.10
  680.6 3.1 collective-permute-done.12
  685.0 3.9 collective-permute-start.19
  689.1 2.8 maximum_convert_fusion
  691.8 6.0 copy.535
  (419 shorter events, 180.8 us)
Async XLA Ops:
  4.4 116.4 %all-to-all-start = ((bf16[8,48,1024]{2,1,0:T(8,128)(2,1)}), bf16[8,48,1024]{2,1,0:T(8,128)(2,1)S(1)}, u32[]{:S(2)}, u32[]{:S(2)}) async-start(bf16[8,48,1024]{2,1,0:T(8,128)(2,1)} %get-tuple-element.173), calls=%async_computation | async-start | bytes 1572864 | tf_op jit(solution)/shard_map/all_to_all | solution.py:604
  152.2 30.4 %all-to-all-start.1 = ((bf16[8,384,384]{2,1,0:T(8,128)(2,1)}), bf16[8,384,384]{2,1,0:T(8,128)(2,1)}, u32[]{:S(2)}, u32[]{:S(2)}) async-start(bf16[8,384,384]{2,1,0:T(8,128)(2,1)} %copy.463), calls=%async_computation.1 | async-start | bytes 4718592 | tf_op jit(solution)/shard_map/all_to_all | solution.py:604
  182.6 42.6 %all-to-all-start.4 = ((bf16[8,48,1024]{2,1,0:T(8,128)(2,1)}), bf16[8,48,1024]{2,1,0:T(8,128)(2,1)S(1)}, u32[]{:S(2)}, u32[]{:S(2)}) async-start(bf16[8,48,1024]{2,1,0:T(8,128)(2,1)} %get-tuple-element.172), calls=%async_computation.4 | async-start | bytes 1572864 | tf_op jit(solution)/shard_map/all_to_all | solution.py:604
  225.2 14.6 %all-to-all-start.2 = ((bf16[8,384,128]{1,2,0:T(8,128)(2,1)}), bf16[8,384,128]{1,2,0:T(8,128)(2,1)}, u32[]{:S(2)}, u32[]{:S(2)}) async-start(bf16[8,384,128]{1,2,0:T(8,128)(2,1)} %copy.464), calls=%async_computation.2 | async-start | bytes 1572864 | tf_op jit(solution)/shard_map/all_to_all | solution.py:604
  239.9 102.9 %collective-permute-start.20 = (bf16[384,1024]{0,1:T(8,128)(2,1)}, bf16[384,1024]{0,1:T(8,128)(2,1)}, u32[]{:S(2)}, u32[]{:S(2)}) collective-permute-start(bf16[384,1024]{0,1:T(8,128)(2,1)} %bitcast.30), channel_id=1, source_target_pairs={{0,4},{4,0},{8,12},{12,8},{16,20},{20,16},{24,28},{28,24},{1,5},{5... | collective-permute-start | bytes 2359304 | tf_op jit(solution)/shard_map/ppermute | solution.py:474
  294.4 17.4 %collective-permute-start.35 = (f32[1024]{0:T(1024)}, f32[1024]{0:T(1024)}, u32[]{:S(2)}, u32[]{:S(2)}) collective-permute-start(f32[1024]{0:T(1024)} %get-tuple-element.58), channel_id=1, source_target_pairs={{0,4},{4,0},{8,12},{12,8},{16,20},{20,16},{24,28},{28,24},{1,5},{5... | collective-permute-start | bytes 12296 | tf_op jit(solution)/shard_map/ppermute | solution.py:474
  296.4 148.3 %collective-permute-start.40 = (bf16[384,1024]{1,0:T(8,128)(2,1)}, bf16[384,1024]{1,0:T(8,128)(2,1)}, u32[]{:S(2)}, u32[]{:S(2)}) collective-permute-start(bf16[384,1024]{1,0:T(8,128)(2,1)} %multiply_convert_fusion.2), channel_id=1, source_target_pairs={{0,4},{4,0},{8,12},{12,8},{16,20},{20,16},{24,28},{28,24},{1,5},{5... | collective-permute-start | bytes 2359304 | tf_op jit(solution)/shard_map/ppermute | solution.py:474
  302.7 70.7 %all-to-all-start.5 = ((bf16[8,384,128]{2,1,0:T(8,128)(2,1)}), bf16[8,384,128]{2,1,0:T(8,128)(2,1)}, u32[]{:S(2)}, u32[]{:S(2)}) async-start(bf16[8,384,128]{2,1,0:T(8,128)(2,1)} %bitcast.573), calls=%async_computation.5 | async-start | bytes 1572864 | tf_op jit(solution)/shard_map/all_to_all | solution.py:604
  307.3 35.5 %collective-permute-start.21 = (bf16[384,512]{1,0:T(8,128)(2,1)}, bf16[384,512]{1,0:T(8,128)(2,1)}, u32[]{:S(2)}, u32[]{:S(2)}) collective-permute-start(bf16[384,512]{1,0:T(8,128)(2,1)} %get-tuple-element.115), channel_id=1, source_target_pairs={{0,4},{4,0},{8,12},{12,8},{16,20},{20,16},{24,28},{28,24},{1,5},{5... | collective-permute-start | bytes 1179656 | tf_op jit(solution)/shard_map/ppermute | solution.py:474
  311.5 129.2 %collective-permute-start.41 = (bf16[384,2624]{0,1:T(8,128)(2,1)}, bf16[384,2624]{0,1:T(8,128)(2,1)}, u32[]{:S(2)}, u32[]{:S(2)}) collective-permute-start(bf16[384,2624]{0,1:T(8,128)(2,1)} %copy.501), channel_id=1, source_target_pairs={{0,4},{4,0},{8,12},{12,8},{16,20},{20,16},{24,28},{28,24},{1,5},{5... | collective-permute-start | bytes 6045704 | tf_op jit(solution)/shard_map/ppermute | solution.py:474
  312.5 5.7 collective-permute-start.36
  325.5 6.4 collective-permute-start.38
  337.7 145.6 %collective-permute-start.55 = (bf16[384,2624]{0,1:T(8,128)(2,1)}, bf16[384,2624]{0,1:T(8,128)(2,1)}, u32[]{:S(2)}, u32[]{:S(2)}) collective-permute-start(bf16[384,2624]{0,1:T(8,128)(2,1)} %copy.514), channel_id=1, source_target_pairs={{0,4},{4,0},{8,12},{12,8},{16,20},{20,16},{24,28},{28,24},{1,5},{5... | collective-permute-start | bytes 6045704 | tf_op jit(solution)/shard_map/ppermute | solution.py:474
  345.3 7.9 %collective-permute-start.28 = (bf16[2,2,2,32,512]{4,3,2,1,0:T(8,128)(2,1)S(1)}, bf16[2,2,2,32,512]{4,3,2,1,0:T(8,128)(2,1)S(1)}, u32[]{:S(2)}, u32[]{:S(2)}) collective-permute-start(bf16[2,2,2,32,512]{4,3,2,1,0:T(8,128)(2,1)S(1)} %fusion.89), channel_id=1, source_target_pairs={{0,16},{4,20},{8,24},{12,28},{16,0},{20,4},{24,8},{28,12},{1,17},{... | collective-permute-start | bytes 786440 | tf_op jit(solution)/shard_map/ppermute | solution.py:474
  346.7 7.6 %collective-permute-start.22 = (bf16[2,2,2,32,512]{4,3,0,1,2:T(8,128)(2,1)S(1)}, bf16[2,2,2,32,512]{4,3,0,1,2:T(8,128)(2,1)S(1)}, u32[]{:S(2)}, u32[]{:S(2)}) collective-permute-start(bf16[2,2,2,32,512]{4,3,0,1,2:T(8,128)(2,1)S(1)} %select_bitcast_fusion.14), channel_id=1, source_target_pairs={{0,8},{4,12},{8,0},{12,4},{16,24},{20,28},{24,16},{28,20},{1,9},{5... | collective-permute-start | bytes 786440 | tf_op jit(solution)/shard_map/ppermute | solution.py:474
  353.4 4.3 collective-permute-start.29
  354.5 4.6 collective-permute-start.23
  373.4 57.7 %all-to-all-start.3 = ((bf16[8,48,1024]{2,1,0:T(8,128)(2,1)}), bf16[8,48,1024]{2,1,0:T(8,128)(2,1)}, u32[]{:S(2)}, u32[]{:S(2)}) async-start(bf16[8,48,1024]{2,1,0:T(8,128)(2,1)} %bitcast.593), calls=%async_computation.3 | async-start | bytes 1572864 | tf_op jit(solution)/shard_map/all_to_all | solution.py:604
  384.1 54.5 %collective-permute-start.34 = (bf16[256,512]{1,0:T(8,128)(2,1)S(1)}, bf16[256,512]{1,0:T(8,128)(2,1)}, u32[]{:S(2)}, u32[]{:S(2)}) collective-permute-start(bf16[256,512]{1,0:T(8,128)(2,1)S(1)} %bitcast.591), channel_id=1, source_target_pairs={{0,4},{4,0},{8,12},{12,8},{16,20},{20,16},{24,28},{28,24},{1,5},{5... | collective-permute-start | bytes 786440 | tf_op jit(solution)/shard_map/ppermute | solution.py:474
  431.1 39.8 %all-to-all-start.6 = ((bf16[8,384,384]{1,2,0:T(8,128)(2,1)}), bf16[8,384,384]{1,2,0:T(8,128)(2,1)}, u32[]{:S(2)}, u32[]{:S(2)}) async-start(bf16[8,384,384]{1,2,0:T(8,128)(2,1)} %copy.469), calls=%async_computation.6 | async-start | bytes 4718592 | tf_op jit(solution)/shard_map/all_to_all | solution.py:604
  467.7 77.8 %collective-permute-start.48 = (bf16[2,2,2,32,2624]{4,3,0,1,2:T(8,128)(2,1)}, bf16[2,2,2,32,2624]{4,3,0,1,2:T(8,128)(2,1)}, u32[]{:S(2)}, u32[]{:S(2)}) collective-permute-start(bf16[2,2,2,32,2624]{4,3,0,1,2:T(8,128)(2,1)} %select_bitcast_fusion), channel_id=1, source_target_pairs={{0,16},{4,20},{8,24},{12,28},{16,0},{20,4},{24,8},{28,12},{1,17},{... | collective-permute-start | bytes 4030472 | tf_op jit(solution)/shard_map/ppermute | solution.py:474
  479.7 7.6 %collective-permute-start = (f32[1024]{0:T(1024)S(1)}, f32[1024]{0:T(1024)S(1)}, u32[]{:S(2)}, u32[]{:S(2)}) collective-permute-start(f32[1024]{0:T(1024)S(1)} %get-tuple-element.53), channel_id=1, source_target_pairs={{0,4},{4,0},{8,12},{12,8},{16,20},{20,16},{24,28},{28,24},{1,5},{5... | collective-permute-start | bytes 12296 | tf_op jit(solution)/shard_map/ppermute | solution.py:474
  482.0 67.6 %collective-permute-start.42 = (bf16[2,2,2,32,2624]{4,3,0,1,2:T(8,128)(2,1)}, bf16[2,2,2,32,2624]{4,3,0,1,2:T(8,128)(2,1)}, u32[]{:S(2)}, u32[]{:S(2)}) collective-permute-start(bf16[2,2,2,32,2624]{4,3,0,1,2:T(8,128)(2,1)} %select_bitcast_fusion.1), channel_id=1, source_target_pairs={{0,8},{4,12},{8,0},{12,4},{16,24},{20,28},{24,16},{28,20},{1,9},{5... | collective-permute-start | bytes 4030472 | tf_op jit(solution)/shard_map/ppermute | solution.py:474
  487.3 26.2 %collective-permute-start.1 = (f32[1024]{0:T(1024)S(1)}, f32[1024]{0:T(1024)S(1)}, u32[]{:S(2)}, u32[]{:S(2)}) collective-permute-start(f32[1024]{0:T(1024)S(1)} %add.301), channel_id=1, source_target_pairs={{0,8},{4,12},{8,0},{12,4},{16,24},{20,28},{24,16},{28,20},{1,9},{5... | collective-permute-start | bytes 12296 | tf_op jit(solution)/shard_map/ppermute | solution.py:474
  518.5 12.9 %collective-permute-start.56 = (bf16[384,512]{1,0:T(8,128)(2,1)S(1)}, bf16[384,512]{1,0:T(8,128)(2,1)S(1)}, u32[]{:S(2)}, u32[]{:S(2)}) collective-permute-start(bf16[384,512]{1,0:T(8,128)(2,1)S(1)} %get-tuple-element.113), channel_id=1, source_target_pairs={{0,4},{4,0},{8,12},{12,8},{16,20},{20,16},{24,28},{28,24},{1,5},{5... | collective-permute-start | bytes 1179656 | tf_op jit(solution)/shard_map/ppermute | solution.py:474
  520.3 10.1 %collective-permute-start.4 = (f32[1024]{0:T(1024)S(1)}, f32[1024]{0:T(1024)S(1)}, u32[]{:S(2)}, u32[]{:S(2)}) collective-permute-start(f32[1024]{0:T(1024)S(1)} %add.304), channel_id=1, source_target_pairs={{0,2},{1,3},{2,0},{3,1},{4,6},{5,7},{6,4},{7,5},{8,10},{9,11},{10,... | collective-permute-start | bytes 12296 | tf_op jit(solution)/shard_map/ppermute | solution.py:474
  523.3 29.8 %all-to-all-start.7 = ((bf16[8,48,1024]{2,1,0:T(8,128)(2,1)}), bf16[8,48,1024]{2,1,0:T(8,128)(2,1)}, u32[]{:S(2)}, u32[]{:S(2)}) async-start(bf16[8,48,1024]{2,1,0:T(8,128)(2,1)} %bitcast.46), calls=%async_computation.7 | async-start | bytes 1572864 | tf_op jit(solution)/shard_map/all_to_all | solution.py:604
  530.2 35.4 %collective-permute-start.6 = (bf16[384,1536]{0,1:T(8,128)(2,1)}, bf16[384,1536]{0,1:T(8,128)(2,1)}, u32[]{:S(2)}, u32[]{:S(2)}) collective-permute-start(bf16[384,1536]{0,1:T(8,128)(2,1)} %get-tuple-element.94), channel_id=1, source_target_pairs={{0,4},{4,0},{8,12},{12,8},{16,20},{20,16},{24,28},{28,24},{1,5},{5... | collective-permute-start | bytes 3538952 | tf_op jit(solution)/shard_map/ppermute | solution.py:474
  530.4 34.8 %collective-permute-start.5 = (bf16[384,1024]{1,0:T(8,128)(2,1)}, bf16[384,1024]{1,0:T(8,128)(2,1)}, u32[]{:S(2)}, u32[]{:S(2)}) collective-permute-start(bf16[384,1024]{1,0:T(8,128)(2,1)} %get-tuple-element.109), channel_id=1, source_target_pairs={{0,4},{4,0},{8,12},{12,8},{16,20},{20,16},{24,28},{28,24},{1,5},{5... | collective-permute-start | bytes 2359304 | tf_op jit(solution)/shard_map/ppermute | solution.py:474
  543.2 16.8 %collective-permute-start.63 = (bf16[2,2,2,328,128]{4,3,0,1,2:T(8,128)(2,1)}, bf16[2,2,2,328,128]{4,3,0,1,2:T(8,128)(2,1)}, u32[]{:S(2)}, u32[]{:S(2)}) collective-permute-start(bf16[2,2,2,328,128]{4,3,0,1,2:T(8,128)(2,1)} %select_bitcast_fusion.5), channel_id=1, source_target_pairs={{0,16},{4,20},{8,24},{12,28},{16,0},{20,4},{24,8},{28,12},{1,17},{... | collective-permute-start | bytes 2015240 | tf_op jit(solution)/shard_map/ppermute | solution.py:474
  545.5 17.0 %collective-permute-start.57 = (bf16[2,2,2,328,128]{4,3,2,1,0:T(8,128)(2,1)}, bf16[2,2,2,328,128]{4,3,2,1,0:T(8,128)(2,1)}, u32[]{:S(2)}, u32[]{:S(2)}) collective-permute-start(bf16[2,2,2,328,128]{4,3,2,1,0:T(8,128)(2,1)} %fusion.72), channel_id=1, source_target_pairs={{0,8},{4,12},{8,0},{12,4},{16,24},{20,28},{24,16},{28,20},{1,9},{5... | collective-permute-start | bytes 2015240 | tf_op jit(solution)/shard_map/ppermute | solution.py:474
  549.6 26.9 %collective-permute-start.49 = (bf16[2,2,32,2624]{3,2,0,1:T(8,128)(2,1)}, bf16[2,2,32,2624]{3,2,0,1:T(8,128)(2,1)}, u32[]{:S(2)}, u32[]{:S(2)}) collective-permute-start(bf16[2,2,32,2624]{3,2,0,1:T(8,128)(2,1)} %select_bitcast_fusion.3), channel_id=1, source_target_pairs={{0,8},{4,12},{8,0},{12,4},{16,24},{20,28},{24,16},{28,20},{1,9},{5... | collective-permute-start | bytes 2015240 | tf_op jit(solution)/shard_map/ppermute | solution.py:474
  560.0 19.2 %collective-permute-start.43 = (bf16[2,2,32,2624]{3,2,0,1:T(8,128)(2,1)S(1)}, bf16[2,2,32,2624]{3,2,0,1:T(8,128)(2,1)S(1)}, u32[]{:S(2)}, u32[]{:S(2)}) collective-permute-start(bf16[2,2,32,2624]{3,2,0,1:T(8,128)(2,1)S(1)} %copy-done.26), channel_id=1, source_target_pairs={{0,16},{4,20},{8,24},{12,28},{16,0},{20,4},{24,8},{28,12},{1,17},{... | collective-permute-start | bytes 2015240 | tf_op jit(solution)/shard_map/ppermute | solution.py:474
  562.6 21.1 %collective-permute-start.64 = (bf16[2,2,328,128]{3,2,0,1:T(8,128)(2,1)S(1)}, bf16[2,2,328,128]{3,2,0,1:T(8,128)(2,1)S(1)}, u32[]{:S(2)}, u32[]{:S(2)}) collective-permute-start(bf16[2,2,328,128]{3,2,0,1:T(8,128)(2,1)S(1)} %select_bitcast_fusion.13), channel_id=1, source_target_pairs={{0,8},{4,12},{8,0},{12,4},{16,24},{20,28},{24,16},{28,20},{1,9},{5... | collective-permute-start | bytes 1007624 | tf_op jit(solution)/shard_map/ppermute | solution.py:474
  565.3 19.1 %collective-permute-start.58 = (bf16[2,2,328,128]{3,2,1,0:T(8,128)(2,1)S(1)}, bf16[2,2,328,128]{3,2,1,0:T(8,128)(2,1)S(1)}, u32[]{:S(2)}, u32[]{:S(2)}) collective-permute-start(bf16[2,2,328,128]{3,2,1,0:T(8,128)(2,1)S(1)} %fusion.85), channel_id=1, source_target_pairs={{0,16},{4,20},{8,24},{12,28},{16,0},{20,4},{24,8},{28,12},{1,17},{... | collective-permute-start | bytes 1007624 | tf_op jit(solution)/shard_map/ppermute | solution.py:474
  570.5 69.8 %collective-permute-start.13 = (bf16[2,2,2,32,1536]{4,3,2,1,0:T(8,128)(2,1)S(1)}, bf16[2,2,2,32,1536]{4,3,2,1,0:T(8,128)(2,1)S(1)}, u32[]{:S(2)}, u32[]{:S(2)}) collective-permute-start(bf16[2,2,2,32,1536]{4,3,2,1,0:T(8,128)(2,1)S(1)} %fusion.57), channel_id=1, source_target_pairs={{0,16},{4,20},{8,24},{12,28},{16,0},{20,4},{24,8},{28,12},{1,17},{... | collective-permute-start | bytes 2359304 | tf_op jit(solution)/shard_map/ppermute | solution.py:474
  576.6 64.9 %collective-permute-start.7 = (bf16[2,2,2,32,1536]{4,3,0,1,2:T(8,128)(2,1)S(1)}, bf16[2,2,2,32,1536]{4,3,0,1,2:T(8,128)(2,1)S(1)}, u32[]{:S(2)}, u32[]{:S(2)}) collective-permute-start(bf16[2,2,2,32,1536]{4,3,0,1,2:T(8,128)(2,1)S(1)} %select_bitcast_fusion.2), channel_id=1, source_target_pairs={{0,8},{4,12},{8,0},{12,4},{16,24},{20,28},{24,16},{28,20},{1,9},{5... | collective-permute-start | bytes 2359304 | tf_op jit(solution)/shard_map/ppermute | solution.py:474
  579.2 23.1 %collective-permute-start.50 = (bf16[2,32,2624]{2,1,0:T(8,128)(2,1)S(1)}, bf16[2,32,2624]{2,1,0:T(8,128)(2,1)S(1)}, u32[]{:S(2)}, u32[]{:S(2)}) collective-permute-start(bf16[2,32,2624]{2,1,0:T(8,128)(2,1)S(1)} %select_bitcast_fusion.9), channel_id=1, source_target_pairs={{0,1},{1,0},{2,3},{3,2},{4,5},{5,4},{6,7},{7,6},{8,9},{9,8},{10,11... | collective-permute-start | bytes 1007624 | tf_op jit(solution)/shard_map/ppermute | solution.py:474
  583.7 20.9 %collective-permute-start.44 = (bf16[2,32,2624]{2,1,0:T(8,128)(2,1)S(1)}, bf16[2,32,2624]{2,1,0:T(8,128)(2,1)S(1)}, u32[]{:S(2)}, u32[]{:S(2)}) collective-permute-start(bf16[2,32,2624]{2,1,0:T(8,128)(2,1)S(1)} %select_bitcast_fusion.12), channel_id=1, source_target_pairs={{0,1},{1,0},{2,3},{3,2},{4,5},{5,4},{6,7},{7,6},{8,9},{9,8},{10,11... | collective-permute-start | bytes 1007624 | tf_op jit(solution)/shard_map/ppermute | solution.py:474
  584.4 12.9 %collective-permute-start.65 = (bf16[2,328,128]{2,1,0:T(8,128)(2,1)S(1)}, bf16[2,328,128]{2,1,0:T(8,128)(2,1)S(1)}, u32[]{:S(2)}, u32[]{:S(2)}) collective-permute-start(bf16[2,328,128]{2,1,0:T(8,128)(2,1)S(1)} %select_bitcast_fusion.28), channel_id=1, source_target_pairs={{0,1},{1,0},{2,3},{3,2},{4,5},{5,4},{6,7},{7,6},{8,9},{9,8},{10,11... | collective-permute-start | bytes 503816 | tf_op jit(solution)/shard_map/ppermute | solution.py:474
  597.3 4.5 collective-permute-start.59
  601.8 6.0 collective-permute-start.66
  602.3 12.6 %collective-permute-start.60 = (bf16[328,128]{1,0:T(8,128)(2,1)S(1)}, bf16[328,128]{1,0:T(8,128)(2,1)S(1)}, u32[]{:S(2)}, u32[]{:S(2)}) collective-permute-start(bf16[328,128]{1,0:T(8,128)(2,1)S(1)} %select_bitcast_fusion.43), channel_id=1, source_target_pairs={{0,2},{1,3},{2,0},{3,1},{4,6},{5,7},{6,4},{7,5},{8,10},{9,11},{10,... | collective-permute-start | bytes 251912 | tf_op jit(solution)/shard_map/ppermute | solution.py:474
  604.5 20.0 %collective-permute-start.51 = (bf16[32,2624]{1,0:T(8,128)(2,1)S(1)}, bf16[32,2624]{1,0:T(8,128)(2,1)S(1)}, u32[]{:S(2)}, u32[]{:S(2)}) collective-permute-start(bf16[32,2624]{1,0:T(8,128)(2,1)S(1)} %select_bitcast_fusion.22), channel_id=1, source_target_pairs={{0,2},{1,3},{2,0},{3,1},{4,6},{5,7},{6,4},{7,5},{8,10},{9,11},{10,... | collective-permute-start | bytes 503816 | tf_op jit(solution)/shard_map/ppermute | solution.py:474
  607.8 18.1 %collective-permute-start.45 = (bf16[32,2624]{1,0:T(8,128)(2,1)S(1)}, bf16[32,2624]{1,0:T(8,128)(2,1)S(1)}, u32[]{:S(2)}, u32[]{:S(2)}) collective-permute-start(bf16[32,2624]{1,0:T(8,128)(2,1)S(1)} %select_bitcast_fusion.25), channel_id=1, source_target_pairs={{0,2},{1,3},{2,0},{3,1},{4,6},{5,7},{6,4},{7,5},{8,10},{9,11},{10,... | collective-permute-start | bytes 503816 | tf_op jit(solution)/shard_map/ppermute | solution.py:474
  614.9 5.1 collective-permute-start.67
  623.5 5.0 collective-permute-start.68
  624.6 5.4 collective-permute-start.62
  625.9 12.1 %collective-permute-start.52 = (bf16[32,2624]{1,0:T(8,128)(2,1)S(1)}, bf16[32,2624]{1,0:T(8,128)(2,1)S(1)}, u32[]{:S(2)}, u32[]{:S(2)}) collective-permute-start(bf16[32,2624]{1,0:T(8,128)(2,1)S(1)} %fusion.83), channel_id=1, source_target_pairs={{0,8},{4,12},{8,0},{12,4},{16,24},{20,28},{24,16},{28,20},{1,9},{5... | collective-permute-start | bytes 503816 | tf_op jit(solution)/shard_map/ppermute | solution.py:474
  628.5 9.7 %collective-permute-start.46 = (bf16[32,2624]{1,0:T(8,128)(2,1)S(1)}, bf16[32,2624]{1,0:T(8,128)(2,1)S(1)}, u32[]{:S(2)}, u32[]{:S(2)}) collective-permute-start(bf16[32,2624]{1,0:T(8,128)(2,1)S(1)} %fusion.84), channel_id=1, source_target_pairs={{0,16},{4,20},{8,24},{12,28},{16,0},{20,4},{24,8},{28,12},{1,17},{... | collective-permute-start | bytes 503816 | tf_op jit(solution)/shard_map/ppermute | solution.py:474
  631.0 36.0 %collective-permute-start.69 = (bf16[656,512]{1,0:T(8,128)(2,1)}, bf16[656,512]{1,0:T(8,128)(2,1)}, u32[]{:S(2)}, u32[]{:S(2)}) collective-permute-start(bf16[656,512]{1,0:T(8,128)(2,1)} %copy_bitcast_fusion.1), channel_id=1, source_target_pairs={{0,4},{4,0},{8,12},{12,8},{16,20},{20,16},{24,28},{28,24},{1,5},{5... | collective-permute-start | bytes 2015240 | tf_op jit(solution)/shard_map/ppermute | solution.py:474
  638.1 9.7 %collective-permute-start.53 = (bf16[2,32,2624]{2,1,0:T(8,128)(2,1)S(1)}, bf16[2,32,2624]{2,1,0:T(8,128)(2,1)S(1)}, u32[]{:S(2)}, u32[]{:S(2)}) collective-permute-start(bf16[2,32,2624]{2,1,0:T(8,128)(2,1)S(1)} %pad_maximum_fusion.9), channel_id=1, source_target_pairs={{0,16},{4,20},{8,24},{12,28},{16,0},{20,4},{24,8},{28,12},{1,17},{... | collective-permute-start | bytes 1007624 | tf_op jit(solution)/shard_map/ppermute | solution.py:474
  638.4 9.6 %collective-permute-start.47 = (bf16[2,32,2624]{2,1,0:T(8,128)(2,1)S(1)}, bf16[2,32,2624]{2,1,0:T(8,128)(2,1)S(1)}, u32[]{:S(2)}, u32[]{:S(2)}) collective-permute-start(bf16[2,32,2624]{2,1,0:T(8,128)(2,1)S(1)} %pad_maximum_fusion.8), channel_id=1, source_target_pairs={{0,8},{4,12},{8,0},{12,4},{16,24},{20,28},{24,16},{28,20},{1,9},{5... | collective-permute-start | bytes 1007624 | tf_op jit(solution)/shard_map/ppermute | solution.py:474
  641.4 14.9 %collective-permute-start.14 = (bf16[2,2,32,1536]{3,2,1,0:T(8,128)(2,1)}, bf16[2,2,32,1536]{3,2,1,0:T(8,128)(2,1)S(1)}, u32[]{:S(2)}, u32[]{:S(2)}) collective-permute-start(bf16[2,2,32,1536]{3,2,1,0:T(8,128)(2,1)} %fusion.79), channel_id=1, source_target_pairs={{0,8},{4,12},{8,0},{12,4},{16,24},{20,28},{24,16},{28,20},{1,9},{5... | collective-permute-start | bytes 1179656 | tf_op jit(solution)/shard_map/ppermute | solution.py:474
  642.5 14.0 %collective-permute-start.8 = (bf16[2,2,32,1536]{3,2,0,1:T(8,128)(2,1)}, bf16[2,2,32,1536]{3,2,0,1:T(8,128)(2,1)}, u32[]{:S(2)}, u32[]{:S(2)}) collective-permute-start(bf16[2,2,32,1536]{3,2,0,1:T(8,128)(2,1)} %select_bitcast_fusion.6), channel_id=1, source_target_pairs={{0,16},{4,20},{8,24},{12,28},{16,0},{20,4},{24,8},{28,12},{1,17},{... | collective-permute-start | bytes 1179656 | tf_op jit(solution)/shard_map/ppermute | solution.py:474
  652.0 36.9 %collective-permute-start.54 = (bf16[256,2624]{0,1:T(8,128)(2,1)}, bf16[256,2624]{0,1:T(8,128)(2,1)S(1)}, u32[]{:S(2)}, u32[]{:S(2)}) collective-permute-start(bf16[256,2624]{0,1:T(8,128)(2,1)} %copy.511), channel_id=1, source_target_pairs={{0,4},{4,0},{8,12},{12,8},{16,20},{20,16},{24,28},{28,24},{1,5},{5... | collective-permute-start | bytes 4030472 | tf_op jit(solution)/shard_map/ppermute | solution.py:474
  656.4 5.1 collective-permute-start.15
  657.7 9.1 %collective-permute-start.9 = (bf16[2,32,1536]{2,1,0:T(8,128)(2,1)S(1)}, bf16[2,32,1536]{2,1,0:T(8,128)(2,1)S(1)}, u32[]{:S(2)}, u32[]{:S(2)}) collective-permute-start(bf16[2,32,1536]{2,1,0:T(8,128)(2,1)S(1)} %select_bitcast_fusion.19), channel_id=1, source_target_pairs={{0,1},{1,0},{2,3},{3,2},{4,5},{5,4},{6,7},{7,6},{8,9},{9,8},{10,11... | collective-permute-start | bytes 589832 | tf_op jit(solution)/shard_map/ppermute | solution.py:474
  661.6 13.1 %collective-permute-start.16 = (bf16[32,1536]{1,0:T(8,128)(2,1)S(1)}, bf16[32,1536]{1,0:T(8,128)(2,1)S(1)}, u32[]{:S(2)}, u32[]{:S(2)}) collective-permute-start(bf16[32,1536]{1,0:T(8,128)(2,1)S(1)} %select_bitcast_fusion.34), channel_id=1, source_target_pairs={{0,2},{1,3},{2,0},{3,1},{4,6},{5,7},{6,4},{7,5},{8,10},{9,11},{10,... | collective-permute-start | bytes 294920 | tf_op jit(solution)/shard_map/ppermute | solution.py:474
  666.9 7.7 %collective-permute-start.10 = (bf16[32,1536]{1,0:T(8,128)(2,1)S(1)}, bf16[32,1536]{1,0:T(8,128)(2,1)S(1)}, u32[]{:S(2)}, u32[]{:S(2)}) collective-permute-start(bf16[32,1536]{1,0:T(8,128)(2,1)S(1)} %select_bitcast_fusion.37), channel_id=1, source_target_pairs={{0,2},{1,3},{2,0},{3,1},{4,6},{5,7},{6,4},{7,5},{8,10},{9,11},{10,... | collective-permute-start | bytes 294920 | tf_op jit(solution)/shard_map/ppermute | solution.py:474
  674.8 5.1 collective-permute-start.17
  678.2 5.4 collective-permute-start.12
  680.0 4.9 collective-permute-start.18
  685.0 12.9 %collective-permute-start.19 = (bf16[256,1536]{1,0:T(8,128)(2,1)S(1)}, bf16[256,1536]{1,0:T(8,128)(2,1)S(1)}, u32[]{:S(2)}, u32[]{:S(2)}) collective-permute-start(bf16[256,1536]{1,0:T(8,128)(2,1)S(1)} %bitcast.575), channel_id=1, source_target_pairs={{0,4},{4,0},{8,12},{12,8},{16,20},{20,16},{24,28},{28,24},{1,5},{5... | collective-permute-start | bytes 2359304 | tf_op jit(solution)/shard_map/ppermute | solution.py:474
  (55 other events, 321.4 us)
